TPU v7x, 32 devices: a whole 2x2x4 slice. The times are simulated.
32 devices in a mesh: ax: 4 (over x, core), ay: 8 (over z, y).
Axes of the slice: x: 2, y: 2, z: 4, core: 2. Of those that a mesh axis runs over, the one named last changes fastest.
Arguments:
- matrices: bfloat16 [256, 512, 512], P(('ax', 'ay')), as said below
- basis_cols: bfloat16 [256, 512, 384], P(('ax', 'ay')), may hold values from -6 to 6
- mode_counts: int32 [256], P(('ax', 'ay')), may hold values from 64 to 384
- task_map: int32 [256], P(('ax', 'ay')), may hold values from 0 to 7, as said below
- neighbour: int32 [256], P(('ax', 'ay')), may hold values from 0 to 7
Outputs:
- smoothed: bfloat16 [256, 512, 384], P(('ax', 'ay'))
- coarse: bfloat16 [256, 384, 384], P(('ax', 'ay'))
Inputs may be any that keep to these rules, and one draw needn't show every extreme that they name: `task_map`: each block of 8 consecutive entries (the agglomerates of one device) holds every ay index exactly once. `matrices`: symmetric with a positive diagonal.
All inputs are finite; a program needn't handle non-finite values.
Results may differ from a plain program's by a relative error of at most 0.0066.
Values may be sent and summed in bfloat16 or wider, within the bound.
No kernel may reach another device: no remote copies, remote signals or barrier semaphores. Data moves between devices by JAX's collectives and lax.ppermute only.
A program may use at most 128 MiB of HBM per device.

v0:
```python
import functools
import math

import jax
import jax.numpy as jnp
from jax import lax
from jax.experimental import pallas as pl
from jax.experimental.pallas import tpu as pltpu
from jax.sharding import PartitionSpec as P


TILE = 128
omegas = (0.3, 0.25, 0.2, 0.3, 0.25, 0.2)

SMEM = pl.BlockSpec(memory_space=pltpu.SMEM)
VMEM = pl.BlockSpec(memory_space=pltpu.VMEM)
ANY = pl.BlockSpec(memory_space=pl.ANY)


def limit(mib):
    return pltpu.CompilerParams(vmem_limit_bytes=mib << 20)


def in_hbm(array):
    return pltpu.with_memory_space_constraint(array, pltpu.HBM)


def in_vmem(array):
    return pltpu.with_memory_space_constraint(array, pltpu.VMEM)


class Route:
    def __init__(self, columns):
        half = columns // 2
        self.columns = columns
        self.paired = columns & (columns - 1) == 0
        self.steps = tuple(range(half, columns)) + tuple(range(half - 1, -1, -1))

    def to(self, me, k):
        return me ^ k if self.paired else (me + k) % self.columns

    def back(self, me, k):
        return me ^ k if self.paired else (me - k + self.columns) % self.columns

    def pairs(self, k):
        return [(i, self.to(i, k)) for i in range(self.columns)]

    def slot(self, table, me, j):
        target = self.to(me, self.steps[j])
        found = jnp.int32(0)
        for s in range(self.columns):
            found = jnp.where(table[s] == target, s, found)
        return found


def smooth_kernel(route, cuts, counts, above, me, a_ref, b_ref, x_ref, xv_ref, y_ref, *refs):
    sent, (sems,) = refs[:-1], refs[-1:]
    slots, width, modes = b_ref.shape
    step = pl.program_id(0)
    first = step * slots
    mine = [counts[first + s] for s in range(slots)]
    groups = pl.cdiv(functools.reduce(jnp.maximum, mine), TILE)
    for live in range(1, modes // TILE + 1):

        @pl.when(groups == live)
        def _():
            top = live * TILE
            rows = lax.broadcasted_iota(jnp.int32, (top, width), 0)
            zero = jnp.zeros((), jnp.bfloat16)
            current = [
                jnp.where(rows < mine[s], b_ref[s, :, :top].T, zero) for s in range(slots)
            ]
            for weight in omegas:
                product = [
                    jnp.dot(current[s], a_ref[s], preferred_element_type=jnp.float32)
                    for s in range(slots)
                ]
                current = [
                    (c.astype(jnp.float32) - weight * p).astype(jnp.bfloat16)
                    for c, p in zip(current, product)
                ]
            for s, c in enumerate(current):
                image = jnp.dot(c, a_ref[s], preferred_element_type=jnp.float32)
                y_ref[first + s, :top, :] = image.astype(jnp.bfloat16)
                xv_ref[first + s, :, :top] = c.T
                if top < modes:
                    y_ref[first + s, top:, :] = jnp.zeros((modes - top, width), jnp.bfloat16)
                    xv_ref[first + s, :, top:] = jnp.zeros((width, modes - top), jnp.bfloat16)

    x_ref[...] = xv_ref[pl.ds(first, slots)]

    columns = route.columns
    copies = []
    for out, a, b in zip(sent, cuts[:-1], cuts[1:]):
        for j in range(a, b):
            wanted = above[columns + route.slot(above, me[0], j)]
            copy = pltpu.make_async_copy(xv_ref.at[wanted], out.at[j - a], sems.at[j])
            copies.append(copy)

            @pl.when(wanted // slots == step)
            def _():
                copy.start()

    @pl.when(step == pl.num_programs(0) - 1)
    def _():
        for copy in copies:
            copy.wait()


def smooth(route, cuts, counts, above, me, matrices, basis):
    total, width, modes = basis.shape
    slots = 2 - total % 2
    at = lambda i, *_: (i, 0, 0)
    spans = [b - a for a, b in zip(cuts[:-1], cuts[1:])]
    return pl.pallas_call(
        functools.partial(smooth_kernel, route, cuts),
        grid_spec=pltpu.PrefetchScalarGridSpec(
            num_scalar_prefetch=3,
            grid=(total // slots,),
            in_specs=[
                pl.BlockSpec((slots, width, width), at),
                pl.BlockSpec((slots, width, modes), at),
            ],
            out_specs=[pl.BlockSpec((slots, width, modes), at), VMEM, VMEM] + [ANY] * len(spans),
            scratch_shapes=[pltpu.SemaphoreType.DMA((total,))],
        ),
        out_shape=[
            jax.ShapeDtypeStruct((total, width, modes), jnp.bfloat16),
            pltpu.VMEM((total, width, modes), jnp.bfloat16),
            pltpu.VMEM((total, modes, width), jnp.bfloat16),
        ]
        + [jax.ShapeDtypeStruct((n, width, modes), jnp.bfloat16) for n in spans],
        compiler_params=limit(24),
        cost_estimate=pl.CostEstimate(
            flops=14 * total * width * width * modes,
            bytes_accessed=2 * total * width * (width + 3 * modes),
            transcendentals=0,
        ),
    )(counts, above, me, in_hbm(matrices), in_hbm(basis))


def block_kernel(route, begin, task, me, x_ref, y_ref, low_ref, *outs):
    scale = 1.0 / math.sqrt(x_ref.shape[1])
    for i, out in enumerate(outs):
        g = route.slot(task, me[0], begin + i)
        y = y_ref[g]
        pair = jnp.dot(y, low_ref[i], preferred_element_type=jnp.float32).astype(jnp.bfloat16)
        own = jnp.dot(y, x_ref[g], preferred_element_type=jnp.float32)
        out[0] = ((own + pair.astype(jnp.float32)) * scale).astype(jnp.bfloat16)


def blocks(route, begin, n, task, me, x, y, low):
    _, width, modes = x.shape
    return pl.pallas_call(
        functools.partial(block_kernel, route, begin),
        in_specs=[SMEM, SMEM, VMEM, VMEM, VMEM],
        out_specs=[VMEM] * n,
        out_shape=[jax.ShapeDtypeStruct((1, modes, modes), jnp.bfloat16)] * n,
        compiler_params=limit(16),
        cost_estimate=pl.CostEstimate(
            flops=4 * n * width * modes * modes,
            bytes_accessed=2 * n * modes * (3 * width + modes),
            transcendentals=0,
        ),
    )(task, me, in_vmem(x), in_vmem(y), in_vmem(low))


def place_kernel(route, me, *refs):
    pieces, out, sems = refs[:-2], refs[-2], refs[-1]
    copies = [
        pltpu.make_async_copy(piece.at[0], out.at[route.back(me[0], k)], sems.at[i])
        for i, (k, piece) in enumerate(zip(route.steps, pieces))
    ]
    for copy in copies:
        copy.start()
    for copy in copies:
        copy.wait()


def place(route, me, pieces):
    n = len(pieces)
    modes = pieces[0].shape[1]
    return pl.pallas_call(
        functools.partial(place_kernel, route),
        in_specs=[SMEM] + [VMEM] * n,
        out_specs=ANY,
        out_shape=jax.ShapeDtypeStruct((n, modes, modes), jnp.bfloat16),
        scratch_shapes=[pltpu.SemaphoreType.DMA((n,))],
        compiler_params=limit(8),
        cost_estimate=pl.CostEstimate(
            flops=0, bytes_accessed=4 * n * modes * modes, transcendentals=0
        ),
    )(me, *[in_vmem(piece) for piece in pieces])


def body(matrices, basis_cols, mode_counts, task_map, neighbour):
    columns, rows = lax.axis_size("ay"), lax.axis_size("ax")
    route = Route(columns)
    me = lax.axis_index("ay").astype(jnp.int32).reshape(1)
    down = [(i + 1, i) for i in range(rows - 1)]
    up = [(i, i + 1) for i in range(rows - 1)]
    cuts = (0, columns // 4, columns // 4 + 3 * columns // 8, columns)

    above = lax.ppermute(jnp.concatenate([task_map, neighbour]), "ax", down)
    out, x, y, *sent = smooth(route, cuts, mode_counts, above, me, matrices, basis_cols)
    lows = []
    for chosen in sent:
        lows.append(lax.ppermute(chosen, "ax", up))
    arrived = []
    for a, b, low in zip(cuts[:-1], cuts[1:], lows):
        made = blocks(route, a, b - a, task_map, me, x, y, low)
        for j, block in zip(range(a, b), made):
            if route.steps[j]:
                block = lax.ppermute(block, "ay", route.pairs(route.steps[j]))
            arrived.append(block)
    return out, place(route, me, arrived)


def solution(mesh):
    agg = P(("ax", "ay"), None, None)
    flat = P(("ax", "ay"))
    return jax.shard_map(
        body,
        mesh=mesh,
        in_specs=(agg, agg, flat, flat, flat),
        out_specs=(agg, agg),
        check_vma=False,
    )
```

profile of v0, /device:TPU:2, one launch (start us, length us, event | category | flops | bytes accessed | tf_op | source)
XLA Modules:
  0.0 95.7 jit_solution(11083585549289340086)
XLA Ops:
  0.6 0.7 pad_add_fusion
  1.4 1.9 %collective-permute-start = (s32[16]{0:T(128)S(1)}, s32[16]{0:T(128)S(1)}, u32[]{:S(2)}, u32[]{:S(2)}) collective-permute-start(s32[16]{0:T(128)S(1)} %pad_add_fusion), channel_id=1, source_target_pairs={{8,0},{16,8},{24,16},{9,1},{17,9},{25,17},{10,2},{18,10},{26,18},{... | collective-permute-start | bytes 200 | tf_op jit(solution)/shard_map/ppermute | solution.py:204
  3.3 1.3 %collective-permute-done.above = s32[16]{0:T(128)S(1)} collective-permute-done((s32[16]{0:T(128)S(1)}, s32[16]{0:T(128)S(1)}, u32[]{:S(2)}, u32[]{:S(2)}) %collective-permute-start) | collective-permute-done | bytes 96 | tf_op jit(solution)/shard_map/ppermute | solution.py:204
  4.6 0.0 copy-start.1
  4.6 0.7 copy-done.1
  5.2 0.0 copy-start
  5.2 17.9 %shard_map.68 = (bf16[8,512,384]{2,1,0:T(8,128)(2,1)}, bf16[8,512,384]{2,1,0:T(8,128)(2,1)S(1)}, bf16[8,384,512]{2,1,0:T(8,128)(2,1)S(1)}, bf16[2,512,384]{2,1,0...) custom-call(s32[8]{0:T(128)S(1)} %copy-done.1, s32[16]{0:T(128)S(1)} %collective-permute-done.above, ...), custom_call_target="tpu_custom_call" | custom-call | flops 11274289152 | bytes 13631488 | tf_op jit(solution)/shard_map/pallas_call | solution.py:115
  23.1 1.9 %collective-permute-start.4 = (bf16[3,512,384]{2,1,0:T(8,128)(2,1)S(1)}, bf16[3,512,384]{2,1,0:T(8,128)(2,1)S(1)}, u32[]{:S(2)}, u32[]{:S(2)}) collective-permute-start(bf16[3,512,384]{2,1,0:T(8,128)(2,1)S(1)} %get-tuple-element.22), channel_id=1, source_target_pairs={{0,8},{8,16},{16,24},{1,9},{9,17},{17,25},{2,10},{10,18},{18,26},{... | collective-permute-start | bytes 3538952 | tf_op jit(solution)/shard_map/ppermute | solution.py:208
  25.1 1.9 %collective-permute-start.8 = (bf16[3,512,384]{2,1,0:T(8,128)(2,1)S(1)}, bf16[3,512,384]{2,1,0:T(8,128)(2,1)S(1)}, u32[]{:S(2)}, u32[]{:S(2)}) collective-permute-start(bf16[3,512,384]{2,1,0:T(8,128)(2,1)S(1)} %get-tuple-element.26), channel_id=1, source_target_pairs={{0,8},{8,16},{16,24},{1,9},{9,17},{17,25},{2,10},{10,18},{18,26},{... | collective-permute-start | bytes 3538952 | tf_op jit(solution)/shard_map/ppermute | solution.py:208
  27.0 1.9 %collective-permute-start.1 = (bf16[2,512,384]{2,1,0:T(8,128)(2,1)S(1)}, bf16[2,512,384]{2,1,0:T(8,128)(2,1)S(1)}, u32[]{:S(2)}, u32[]{:S(2)}) collective-permute-start(bf16[2,512,384]{2,1,0:T(8,128)(2,1)S(1)} %get-tuple-element.19), channel_id=1, source_target_pairs={{0,8},{8,16},{16,24},{1,9},{9,17},{17,25},{2,10},{10,18},{18,26},{... | collective-permute-start | bytes 2359304 | tf_op jit(solution)/shard_map/ppermute | solution.py:208
  28.9 32.8 %collective-permute-done.1.low_ref = bf16[2,512,384]{2,1,0:T(8,128)(2,1)S(1)} collective-permute-done((bf16[2,512,384]{2,1,0:T(8,128)(2,1)S(1)}, bf16[2,512,384]{2,1,0:T(8,128)(2,1)S(1)}, u32[]{:S(2)}, u32[]{:S(2)}) %collective-permute-start.1) | collective-permute-done | bytes 786464 | tf_op jit(solution)/shard_map/ppermute | solution.py:208
  61.7 0.0 copy-done
  61.7 1.5 %shard_map.69 = (bf16[1,384,384]{2,1,0:T(8,128)(2,1)S(1)}, bf16[1,384,384]{2,1,0:T(8,128)(2,1)S(1)}) custom-call(s32[8]{0:T(128)S(1)} %copy-done, s32[1]{0:T(128)} %bitcast.me, bf16[8,512,384]{2,1,0:T(8,128)(2,1)S(1)} %get-tuple-element.17.x_ref, bf16[8,384,512]{2,1,0:T(8,128)(2,1)S(1)} %get-tuple-element.18.y_ref, ...), custom_call_target="tpu_custom_call" | custom-call | flops 603979776 | bytes 2949120 | tf_op jit(solution)/shard_map/pallas_call | solution.py:154
  63.3 1.6 %collective-permute-start.2 = (bf16[1,384,384]{2,1,0:T(8,128)(2,1)S(1)}, bf16[1,384,384]{2,1,0:T(8,128)(2,1)S(1)}, u32[]{:S(2)}, u32[]{:S(2)}) collective-permute-start(bf16[1,384,384]{2,1,0:T(8,128)(2,1)S(1)} %get-tuple-element.20), channel_id=1, source_target_pairs={{0,4},{1,5},{2,6},{3,7},{4,0},{5,1},{6,2},{7,3},{8,12},{9,13},{10,... | collective-permute-start | bytes 884744 | tf_op jit(solution)/shard_map/ppermute | solution.py:214
  64.9 2.3 %collective-permute-start.3 = (bf16[1,384,384]{2,1,0:T(8,128)(2,1)S(1)}, bf16[1,384,384]{2,1,0:T(8,128)(2,1)S(1)}, u32[]{:S(2)}, u32[]{:S(2)}) collective-permute-start(bf16[1,384,384]{2,1,0:T(8,128)(2,1)S(1)} %get-tuple-element.21), channel_id=1, source_target_pairs={{0,5},{1,4},{2,7},{3,6},{4,1},{5,0},{6,3},{7,2},{8,13},{9,12},{10,... | collective-permute-start | bytes 884744 | tf_op jit(solution)/shard_map/ppermute | solution.py:214
  67.2 0.0 collective-permute-done.4.low_ref
  67.2 1.9 %shard_map.70 = (bf16[1,384,384]{2,1,0:T(8,128)(2,1)S(1)}, bf16[1,384,384]{2,1,0:T(8,128)(2,1)S(1)}, bf16[1,384,384]{2,1,0:T(8,128)(2,1)S(1)}) custom-call(s32[8]{0:T(128)S(1)} %copy-done, s32[1]{0:T(128)} %bitcast.me, bf16[8,512,384]{2,1,0:T(8,128)(2,1)S(1)} %get-tuple-element.17.x_ref, bf16[8,384,512]{2,1,0:T(8,128)(2,1)S(1)} %get-tuple-element.18.y_ref, ...), custom_call_target="tpu_custom_call" | custom-call | flops 905969664 | bytes 4423680 | tf_op jit(solution)/shard_map/pallas_call | solution.py:154
  69.1 2.7 %collective-permute-start.5 = (bf16[1,384,384]{2,1,0:T(8,128)(2,1)S(1)}, bf16[1,384,384]{2,1,0:T(8,128)(2,1)S(1)}, u32[]{:S(2)}, u32[]{:S(2)}) collective-permute-start(bf16[1,384,384]{2,1,0:T(8,128)(2,1)S(1)} %get-tuple-element.23), channel_id=1, source_target_pairs={{0,6},{1,7},{2,4},{3,5},{4,2},{5,3},{6,0},{7,1},{8,14},{9,15},{10,... | collective-permute-start | bytes 884744 | tf_op jit(solution)/shard_map/ppermute | solution.py:214
  71.8 1.1 %collective-permute-start.6 = (bf16[1,384,384]{2,1,0:T(8,128)(2,1)S(1)}, bf16[1,384,384]{2,1,0:T(8,128)(2,1)S(1)}, u32[]{:S(2)}, u32[]{:S(2)}) collective-permute-start(bf16[1,384,384]{2,1,0:T(8,128)(2,1)S(1)} %get-tuple-element.24), channel_id=1, source_target_pairs={{0,7},{1,6},{2,5},{3,4},{4,3},{5,2},{6,1},{7,0},{8,15},{9,14},{10,... | collective-permute-start | bytes 884744 | tf_op jit(solution)/shard_map/ppermute | solution.py:214
  73.0 0.0 collective-permute-done.8.low_ref
  73.0 0.3 collective-permute-start.7
  73.3 1.9 %shard_map.71 = (bf16[1,384,384]{2,1,0:T(8,128)(2,1)S(1)}, bf16[1,384,384]{2,1,0:T(8,128)(2,1)S(1)}, bf16[1,384,384]{2,1,0:T(8,128)(2,1)S(1)}) custom-call(s32[8]{0:T(128)S(1)} %copy-done, s32[1]{0:T(128)} %bitcast.me, bf16[8,512,384]{2,1,0:T(8,128)(2,1)S(1)} %get-tuple-element.17.x_ref, bf16[8,384,512]{2,1,0:T(8,128)(2,1)S(1)} %get-tuple-element.18.y_ref, ...), custom_call_target="tpu_custom_call" | custom-call | flops 905969664 | bytes 4423680 | tf_op jit(solution)/shard_map/pallas_call | solution.py:154
  75.2 8.4 %collective-permute-done.2.refs_0_ = bf16[1,384,384]{2,1,0:T(8,128)(2,1)S(1)} collective-permute-done((bf16[1,384,384]{2,1,0:T(8,128)(2,1)S(1)}, bf16[1,384,384]{2,1,0:T(8,128)(2,1)S(1)}, u32[]{:S(2)}, u32[]{:S(2)}) %collective-permute-start.2) | collective-permute-done | bytes 294944 | tf_op jit(solution)/shard_map/ppermute | solution.py:214
  83.7 0.0 collective-permute-start.9
  83.7 3.8 %collective-permute-done.3.refs_1_ = bf16[1,384,384]{2,1,0:T(8,128)(2,1)S(1)} collective-permute-done((bf16[1,384,384]{2,1,0:T(8,128)(2,1)S(1)}, bf16[1,384,384]{2,1,0:T(8,128)(2,1)S(1)}, u32[]{:S(2)}, u32[]{:S(2)}) %collective-permute-start.3) | collective-permute-done | bytes 294944 | tf_op jit(solution)/shard_map/ppermute | solution.py:214
  87.5 0.8 collective-permute-start.10
  88.3 0.0 collective-permute-done.5.refs_2_
  88.3 0.0 collective-permute-done.6.refs_3_
  88.3 2.3 %collective-permute-done.7.refs_4_ = bf16[1,384,384]{2,1,0:T(8,128)(2,1)S(1)} collective-permute-done((bf16[1,384,384]{2,1,0:T(8,128)(2,1)S(1)}, bf16[1,384,384]{2,1,0:T(8,128)(2,1)S(1)}, u32[]{:S(2)}, u32[]{:S(2)}) %collective-permute-start.7) | collective-permute-done | bytes 294944 | tf_op jit(solution)/shard_map/ppermute | solution.py:214
  90.6 2.5 %collective-permute-done.9.refs_5_ = bf16[1,384,384]{2,1,0:T(8,128)(2,1)S(1)} collective-permute-done((bf16[1,384,384]{2,1,0:T(8,128)(2,1)S(1)}, bf16[1,384,384]{2,1,0:T(8,128)(2,1)S(1)}, u32[]{:S(2)}, u32[]{:S(2)}) %collective-permute-start.9) | collective-permute-done | bytes 294944 | tf_op jit(solution)/shard_map/ppermute | solution.py:214
  93.1 1.2 %collective-permute-done.10.refs_6_ = bf16[1,384,384]{2,1,0:T(8,128)(2,1)S(1)} collective-permute-done((bf16[1,384,384]{2,1,0:T(8,128)(2,1)S(1)}, bf16[1,384,384]{2,1,0:T(8,128)(2,1)S(1)}, u32[]{:S(2)}, u32[]{:S(2)}) %collective-permute-start.10) | collective-permute-done | bytes 294944 | tf_op jit(solution)/shard_map/ppermute | solution.py:214
  94.2 1.5 %shard_map.72 = bf16[8,384,384]{2,1,0:T(8,128)(2,1)} custom-call(s32[1]{0:T(128)} %bitcast.me, bf16[1,384,384]{2,1,0:T(8,128)(2,1)S(1)} %collective-permute-done.2.refs_0_, bf16[1,384,384]{2,1,0:T(8,128)(2,1)S(1)} %collective-permute-done.3.refs_1_, bf16[1,384,384]{2,1,0:T(8,128)(2,1)S(1)} %collective-permute-done.5.refs_2_, ...), custom_call_target="tpu_custom_call" | custom-call | bytes 4718592 | tf_op jit(solution)/shard_map/pallas_call | solution.py:183
Async XLA Ops:
  1.4 3.2 %collective-permute-start = (s32[16]{0:T(128)S(1)}, s32[16]{0:T(128)S(1)}, u32[]{:S(2)}, u32[]{:S(2)}) collective-permute-start(s32[16]{0:T(128)S(1)} %pad_add_fusion), channel_id=1, source_target_pairs={{8,0},{16,8},{24,16},{9,1},{17,9},{25,17},{10,2},{18,10},{26,18},{... | collective-permute-start | bytes 200 | tf_op jit(solution)/shard_map/ppermute | solution.py:204
  4.6 0.7 copy-start.1
  5.2 56.5 %copy-start = (s32[8]{0:T(128)S(1)}, s32[8]{0:T(128)}, u32[]{:S(2)}) copy-start(s32[8]{0:T(128)} %task.5) | copy-start | bytes 100
  23.1 44.0 %collective-permute-start.4 = (bf16[3,512,384]{2,1,0:T(8,128)(2,1)S(1)}, bf16[3,512,384]{2,1,0:T(8,128)(2,1)S(1)}, u32[]{:S(2)}, u32[]{:S(2)}) collective-permute-start(bf16[3,512,384]{2,1,0:T(8,128)(2,1)S(1)} %get-tuple-element.22), channel_id=1, source_target_pairs={{0,8},{8,16},{16,24},{1,9},{9,17},{17,25},{2,10},{10,18},{18,26},{... | collective-permute-start | bytes 3538952 | tf_op jit(solution)/shard_map/ppermute | solution.py:208
  25.1 47.9 %collective-permute-start.8 = (bf16[3,512,384]{2,1,0:T(8,128)(2,1)S(1)}, bf16[3,512,384]{2,1,0:T(8,128)(2,1)S(1)}, u32[]{:S(2)}, u32[]{:S(2)}) collective-permute-start(bf16[3,512,384]{2,1,0:T(8,128)(2,1)S(1)} %get-tuple-element.26), channel_id=1, source_target_pairs={{0,8},{8,16},{16,24},{1,9},{9,17},{17,25},{2,10},{10,18},{18,26},{... | collective-permute-start | bytes 3538952 | tf_op jit(solution)/shard_map/ppermute | solution.py:208
  27.0 34.7 %collective-permute-start.1 = (bf16[2,512,384]{2,1,0:T(8,128)(2,1)S(1)}, bf16[2,512,384]{2,1,0:T(8,128)(2,1)S(1)}, u32[]{:S(2)}, u32[]{:S(2)}) collective-permute-start(bf16[2,512,384]{2,1,0:T(8,128)(2,1)S(1)} %get-tuple-element.19), channel_id=1, source_target_pairs={{0,8},{8,16},{16,24},{1,9},{9,17},{17,25},{2,10},{10,18},{18,26},{... | collective-permute-start | bytes 2359304 | tf_op jit(solution)/shard_map/ppermute | solution.py:208
  63.3 20.4 %collective-permute-start.2 = (bf16[1,384,384]{2,1,0:T(8,128)(2,1)S(1)}, bf16[1,384,384]{2,1,0:T(8,128)(2,1)S(1)}, u32[]{:S(2)}, u32[]{:S(2)}) collective-permute-start(bf16[1,384,384]{2,1,0:T(8,128)(2,1)S(1)} %get-tuple-element.20), channel_id=1, source_target_pairs={{0,4},{1,5},{2,6},{3,7},{4,0},{5,1},{6,2},{7,3},{8,12},{9,13},{10,... | collective-permute-start | bytes 884744 | tf_op jit(solution)/shard_map/ppermute | solution.py:214
  64.9 22.6 %collective-permute-start.3 = (bf16[1,384,384]{2,1,0:T(8,128)(2,1)S(1)}, bf16[1,384,384]{2,1,0:T(8,128)(2,1)S(1)}, u32[]{:S(2)}, u32[]{:S(2)}) collective-permute-start(bf16[1,384,384]{2,1,0:T(8,128)(2,1)S(1)} %get-tuple-element.21), channel_id=1, source_target_pairs={{0,5},{1,4},{2,7},{3,6},{4,1},{5,0},{6,3},{7,2},{8,13},{9,12},{10,... | collective-permute-start | bytes 884744 | tf_op jit(solution)/shard_map/ppermute | solution.py:214
  69.1 19.2 %collective-permute-start.5 = (bf16[1,384,384]{2,1,0:T(8,128)(2,1)S(1)}, bf16[1,384,384]{2,1,0:T(8,128)(2,1)S(1)}, u32[]{:S(2)}, u32[]{:S(2)}) collective-permute-start(bf16[1,384,384]{2,1,0:T(8,128)(2,1)S(1)} %get-tuple-element.23), channel_id=1, source_target_pairs={{0,6},{1,7},{2,4},{3,5},{4,2},{5,3},{6,0},{7,1},{8,14},{9,15},{10,... | collective-permute-start | bytes 884744 | tf_op jit(solution)/shard_map/ppermute | solution.py:214
  71.8 16.5 %collective-permute-start.6 = (bf16[1,384,384]{2,1,0:T(8,128)(2,1)S(1)}, bf16[1,384,384]{2,1,0:T(8,128)(2,1)S(1)}, u32[]{:S(2)}, u32[]{:S(2)}) collective-permute-start(bf16[1,384,384]{2,1,0:T(8,128)(2,1)S(1)} %get-tuple-element.24), channel_id=1, source_target_pairs={{0,7},{1,6},{2,5},{3,4},{4,3},{5,2},{6,1},{7,0},{8,15},{9,14},{10,... | collective-permute-start | bytes 884744 | tf_op jit(solution)/shard_map/ppermute | solution.py:214
  73.0 17.6 %collective-permute-start.7 = (bf16[1,384,384]{2,1,0:T(8,128)(2,1)S(1)}, bf16[1,384,384]{2,1,0:T(8,128)(2,1)S(1)}, u32[]{:S(2)}, u32[]{:S(2)}) collective-permute-start(bf16[1,384,384]{2,1,0:T(8,128)(2,1)S(1)} %get-tuple-element.25), channel_id=1, source_target_pairs={{0,3},{1,2},{2,1},{3,0},{4,7},{5,6},{6,5},{7,4},{8,11},{9,10},{10,... | collective-permute-start | bytes 884744 | tf_op jit(solution)/shard_map/ppermute | solution.py:214
  83.7 9.4 %collective-permute-start.9 = (bf16[1,384,384]{2,1,0:T(8,128)(2,1)S(1)}, bf16[1,384,384]{2,1,0:T(8,128)(2,1)S(1)}, u32[]{:S(2)}, u32[]{:S(2)}) collective-permute-start(bf16[1,384,384]{2,1,0:T(8,128)(2,1)S(1)} %get-tuple-element.27), channel_id=1, source_target_pairs={{0,2},{1,3},{2,0},{3,1},{4,6},{5,7},{6,4},{7,5},{8,10},{9,11},{10,... | collective-permute-start | bytes 884744 | tf_op jit(solution)/shard_map/ppermute | solution.py:214
  87.5 6.7 %collective-permute-start.10 = (bf16[1,384,384]{2,1,0:T(8,128)(2,1)S(1)}, bf16[1,384,384]{2,1,0:T(8,128)(2,1)S(1)}, u32[]{:S(2)}, u32[]{:S(2)}) collective-permute-start(bf16[1,384,384]{2,1,0:T(8,128)(2,1)S(1)} %get-tuple-element.28), channel_id=1, source_target_pairs={{0,1},{1,0},{2,3},{3,2},{4,5},{5,4},{6,7},{7,6},{8,9},{9,8},{10,11... | collective-permute-start | bytes 884744 | tf_op jit(solution)/shard_map/ppermute | solution.py:214
where the time goes:
time: 96.6 us; the launch traced here: 95.7 us
  waiting for transfers between devices  52.3 us (54%)
  Pallas kernels  24.7 us (26%)
  starting transfers between devices  16.6 us (17%)
    ppermute x3, waiting for transfers between devices, body(): lows.append(lax.ppermute(chosen, 'ax', up))  32.8 us
    ppermute x7, waiting for transfers between devices, body(): block = lax.ppermute(block, 'ay', route.pairs(route.steps[j]))  18.2 us
    pallas_call x1, Pallas kernels, smooth(): pl.pallas_call(functools.partial(smooth_kernel, route, cuts), grid_spec=p...  17.9 us
    ppermute x7, starting transfers between devices, body(): block = lax.ppermute(block, 'ay', route.pairs(route.steps[j]))  8.9 us
    ppermute x3, starting transfers between devices, body(): lows.append(lax.ppermute(chosen, 'ax', up))  5.76 us
    pallas_call x3, Pallas kernels, blocks(): pl.pallas_call(functools.partial(block_kernel, route, begin), in_specs=[S...  5.37 us
  transfers between devices with their start and end apart: 11, of which 7 were waited for; matrix products, arithmetic and copies ran while one was open for 0% of the time, Pallas kernels for 6%

commit v1 on v0

--- a/solution.py
+++ b/solution.py
@@ -53,90 +53,143 @@
         return found
 
 
-def smooth_kernel(route, cuts, counts, above, me, a_ref, b_ref, x_ref, xv_ref, y_ref, *refs):
-    sent, (sems,) = refs[:-1], refs[-1:]
-    slots, width, modes = b_ref.shape
-    step = pl.program_id(0)
-    first = step * slots
-    mine = [counts[first + s] for s in range(slots)]
-    groups = pl.cdiv(functools.reduce(jnp.maximum, mine), TILE)
-    for live in range(1, modes // TILE + 1):
-
-        @pl.when(groups == live)
-        def _():
-            top = live * TILE
-            rows = lax.broadcasted_iota(jnp.int32, (top, width), 0)
-            zero = jnp.zeros((), jnp.bfloat16)
-            current = [
-                jnp.where(rows < mine[s], b_ref[s, :, :top].T, zero) for s in range(slots)
-            ]
-            for weight in omegas:
-                product = [
-                    jnp.dot(current[s], a_ref[s], preferred_element_type=jnp.float32)
-                    for s in range(slots)
-                ]
-                current = [
-                    (c.astype(jnp.float32) - weight * p).astype(jnp.bfloat16)
-                    for c, p in zip(current, product)
-                ]
-            for s, c in enumerate(current):
-                image = jnp.dot(c, a_ref[s], preferred_element_type=jnp.float32)
-                y_ref[first + s, :top, :] = image.astype(jnp.bfloat16)
-                xv_ref[first + s, :, :top] = c.T
-                if top < modes:
-                    y_ref[first + s, top:, :] = jnp.zeros((modes - top, width), jnp.bfloat16)
-                    xv_ref[first + s, :, top:] = jnp.zeros((width, modes - top), jnp.bfloat16)
-
-    x_ref[...] = xv_ref[pl.ds(first, slots)]
-
+def arrange(route, early, above, task, me, order):
     columns = route.columns
-    copies = []
+    needed = [route.slot(task, me[0], j) for j in range(early)]
+    needed += [above[columns + route.slot(above, me[0], j)] for j in range(early)]
+    first = [
+        functools.reduce(jnp.maximum, [(n == s).astype(jnp.int32) for n in needed])
+        for s in range(columns)
+    ]
+    ahead, behind = jnp.int32(0), functools.reduce(jnp.add, first)
+    for s in range(columns):
+        order[jnp.where(first[s] > 0, ahead, behind)] = s
+        ahead, behind = ahead + first[s], behind + 1 - first[s]
+
+
+def smooth_kernel(route, early, begin, n, cuts, above, task, me, counts, a_hbm, b_hbm, *refs):
+    chunks = len(cuts) - 1
+    refs = refs[3:] if begin else refs
+    x_ref, xv_ref, y_ref = refs[:3]
+    sent = refs[3 : 3 + chunks]
+    order, a_buf, b_buf, in_sems, out_sems, sent_sems = refs[3 + chunks :]
+    width, modes = b_buf.shape[1:]
+    columns = route.columns
+    arrange(route, early, above, task, me, order)
+
+    def loads(p):
+        g = order[begin + p]
+        return (
+            pltpu.make_async_copy(a_hbm.at[g], a_buf.at[p], in_sems.at[0, p]),
+            pltpu.make_async_copy(b_hbm.at[g], b_buf.at[p], in_sems.at[1, p]),
+        )
+
+    for p in range(n):
+        for copy in loads(p):
+            copy.start()
+
+    wanted, emits = [], []
     for out, a, b in zip(sent, cuts[:-1], cuts[1:]):
         for j in range(a, b):
-            wanted = above[columns + route.slot(above, me[0], j)]
-            copy = pltpu.make_async_copy(xv_ref.at[wanted], out.at[j - a], sems.at[j])
-            copies.append(copy)
-
-            @pl.when(wanted // slots == step)
+            w = above[columns + route.slot(above, me[0], j)]
+            wanted.append(w)
+            emits.append(
+                pltpu.make_async_copy(xv_ref.at[w], out.at[j - a], sent_sems.at[j - cuts[0]])
+            )
+    for w, emit in zip(wanted, emits):
+        if begin:
+            known = functools.reduce(jnp.logical_or, [order[p] == w for p in range(begin)])
+
+            @pl.when(known)
             def _():
-                copy.start()
-
-    @pl.when(step == pl.num_programs(0) - 1)
-    def _():
-        for copy in copies:
-            copy.wait()
-
-
-def smooth(route, cuts, counts, above, me, matrices, basis):
+                emit.start()
+
+    def stored(p):
+        g = order[begin + p]
+        return pltpu.make_async_copy(xv_ref.at[g], x_ref.at[g], out_sems.at[p])
+
+    @pl.loop(0, n // 2)
+    def _(i):
+        at = [2 * i, 2 * i + 1]
+        slots = [order[begin + p] for p in at]
+        for p in at:
+            for copy in loads(p):
+                copy.wait()
+        mine = [counts[g] for g in slots]
+        groups = pl.cdiv(jnp.maximum(*mine), TILE)
+        for live in range(1, modes // TILE + 1):
+
+            @pl.when(groups == live)
+            def _():
+                top = live * TILE
+                rows = lax.broadcasted_iota(jnp.int32, (top, width), 0)
+                zero = jnp.zeros((), jnp.bfloat16)
+                current = [
+                    jnp.where(rows < count, b_buf[p, :, :top].T, zero)
+                    for p, count in zip(at, mine)
+                ]
+                for weight in omegas:
+                    product = [
+                        jnp.dot(c, a_buf[p], preferred_element_type=jnp.float32)
+                        for p, c in zip(at, current)
+                    ]
+                    current = [
+                        (c.astype(jnp.float32) - weight * d).astype(jnp.bfloat16)
+                        for c, d in zip(current, product)
+                    ]
+                for p, g, c in zip(at, slots, current):
+                    image = jnp.dot(c, a_buf[p], preferred_element_type=jnp.float32)
+                    y_ref[g, :top, :] = image.astype(jnp.bfloat16)
+                    xv_ref[g, :, :top] = c.T
+                    if top < modes:
+                        y_ref[g, top:, :] = jnp.zeros((modes - top, width), jnp.bfloat16)
+                        xv_ref[g, :, top:] = jnp.zeros((width, modes - top), jnp.bfloat16)
+
+        for p in at:
+            stored(p).start()
+        for w, emit in zip(wanted, emits):
+
+            @pl.when(jnp.logical_or(w == slots[0], w == slots[1]))
+            def _():
+                emit.start()
+
+    for p in range(n):
+        stored(p).wait()
+    for emit in emits:
+        emit.wait()
+
+
+def smooth(route, early, begin, n, cuts, above, task, me, counts, matrices, basis, before):
     total, width, modes = basis.shape
-    slots = 2 - total % 2
-    at = lambda i, *_: (i, 0, 0)
     spans = [b - a for a, b in zip(cuts[:-1], cuts[1:])]
+    if before:
+        before = [before[0], in_vmem(before[1]), in_vmem(before[2])]
     return pl.pallas_call(
-        functools.partial(smooth_kernel, route, cuts),
-        grid_spec=pltpu.PrefetchScalarGridSpec(
-            num_scalar_prefetch=3,
-            grid=(total // slots,),
-            in_specs=[
-                pl.BlockSpec((slots, width, width), at),
-                pl.BlockSpec((slots, width, modes), at),
-            ],
-            out_specs=[pl.BlockSpec((slots, width, modes), at), VMEM, VMEM] + [ANY] * len(spans),
-            scratch_shapes=[pltpu.SemaphoreType.DMA((total,))],
-        ),
+        functools.partial(smooth_kernel, route, early, begin, n, cuts),
+        in_specs=[SMEM] * 4 + [ANY] * 2 + ([ANY, VMEM, VMEM] if before else []),
+        out_specs=[ANY, VMEM, VMEM] + [ANY] * len(spans),
+        scratch_shapes=[
+            pltpu.SMEM((total,), jnp.int32),
+            pltpu.VMEM((n, width, width), jnp.bfloat16),
+            pltpu.VMEM((n, width, modes), jnp.bfloat16),
+            pltpu.SemaphoreType.DMA((2, n)),
+            pltpu.SemaphoreType.DMA((n,)),
+            pltpu.SemaphoreType.DMA((cuts[-1] - cuts[0],)),
+        ],
         out_shape=[
             jax.ShapeDtypeStruct((total, width, modes), jnp.bfloat16),
             pltpu.VMEM((total, width, modes), jnp.bfloat16),
             pltpu.VMEM((total, modes, width), jnp.bfloat16),
         ]
-        + [jax.ShapeDtypeStruct((n, width, modes), jnp.bfloat16) for n in spans],
+        + [jax.ShapeDtypeStruct((m, width, modes), jnp.bfloat16) for m in spans],
+        input_output_aliases={6: 0, 7: 1, 8: 2} if before else {},
         compiler_params=limit(24),
         cost_estimate=pl.CostEstimate(
-            flops=14 * total * width * width * modes,
-            bytes_accessed=2 * total * width * (width + 3 * modes),
+            flops=14 * n * width * width * modes,
+            bytes_accessed=2 * n * width * (width + 3 * modes),
             transcendentals=0,
         ),
-    )(counts, above, me, in_hbm(matrices), in_hbm(basis))
+    )(above, task, me, counts, in_hbm(matrices), in_hbm(basis), *before)
 
 
 def block_kernel(route, begin, task, me, x_ref, y_ref, low_ref, *outs):
@@ -199,12 +252,16 @@
     me = lax.axis_index("ay").astype(jnp.int32).reshape(1)
     down = [(i + 1, i) for i in range(rows - 1)]
     up = [(i, i + 1) for i in range(rows - 1)]
-    cuts = (0, columns // 4, columns // 4 + 3 * columns // 8, columns)
+    early = columns // 4
+    cuts = (0, early, 2 * early, columns)
+    half = columns // 2
 
     above = lax.ppermute(jnp.concatenate([task_map, neighbour]), "ax", down)
-    out, x, y, *sent = smooth(route, cuts, mode_counts, above, me, matrices, basis_cols)
+    scalars = (above, task_map, me, mode_counts, matrices, basis_cols)
+    *kept, first = smooth(route, early, 0, half, cuts[:2], *scalars, [])
+    out, x, y, *others = smooth(route, early, half, half, cuts[1:], *scalars, kept)
     lows = []
-    for chosen in sent:
+    for chosen in [first, *others]:
         lows.append(lax.ppermute(chosen, "ax", up))
     arrived = []
     for a, b, low in zip(cuts[:-1], cuts[1:], lows):

time: 96.6 us -> 91.8 us (0.950)
  the two profiles are of different devices: /device:TPU:2 before, /device:TPU:9 now
where the time goes in v1:
time: 91.8 us; the launch traced here: 91.5 us
  waiting for transfers between devices  45.6 us (50%)
  Pallas kernels  26.6 us (29%)
  starting transfers between devices  16.4 us (18%)
  local copies, waits for them, and re-layouts  1.32 us (1%)
    ppermute x3, waiting for transfers between devices, body(): lows.append(lax.ppermute(chosen, 'ax', up))  27.6 us
    pallas_call x2, Pallas kernels, smooth(): pl.pallas_call(functools.partial(smooth_kernel, route, early, begin, n, c...  19.8 us
    ppermute x7, waiting for transfers between devices, body(): block = lax.ppermute(block, 'ay', route.pairs(route.steps[j]))  15.7 us
    ppermute x7, starting transfers between devices, body(): block = lax.ppermute(block, 'ay', route.pairs(route.steps[j]))  8.03 us
    ppermute x3, starting transfers between devices, body(): lows.append(lax.ppermute(chosen, 'ax', up))  5.76 us
    pallas_call x3, Pallas kernels, blocks(): pl.pallas_call(functools.partial(block_kernel, route, begin), in_specs=[S...  5.37 us
    ppermute x1, starting transfers between devices, body(): above = lax.ppermute(jnp.concatenate([task_map, neighbour]), 'ax', down)  2.57 us
    ppermute x1, waiting for transfers between devices, body(): above = lax.ppermute(jnp.concatenate([task_map, neighbour]), 'ax', down)  2.33 us
  transfers between devices with their start and end apart: 11, of which 8 were waited for; matrix products, arithmetic and copies ran while one was open for 0% of the time, Pallas kernels for 6%

profile of v1, /device:TPU:9, one launch (start us, length us, event | category | flops | bytes accessed | tf_op | source)
XLA Modules:
  0.0 91.5 jit_solution(17809532737937018338)
XLA Ops:
  0.6 0.7 pad_add_fusion
  1.4 2.6 %collective-permute-start = (s32[16]{0:T(128)S(1)}, s32[16]{0:T(128)S(1)}, u32[]{:S(2)}, u32[]{:S(2)}) collective-permute-start(s32[16]{0:T(128)S(1)} %pad_add_fusion), channel_id=1, source_target_pairs={{8,0},{16,8},{24,16},{9,1},{17,9},{25,17},{10,2},{18,10},{26,18},{... | collective-permute-start | bytes 200 | tf_op jit(solution)/shard_map/ppermute | solution.py:259
  4.0 2.3 %collective-permute-done.above = s32[16]{0:T(128)S(1)} collective-permute-done((s32[16]{0:T(128)S(1)}, s32[16]{0:T(128)S(1)}, u32[]{:S(2)}, u32[]{:S(2)}) %collective-permute-start) | collective-permute-done | bytes 96 | tf_op jit(solution)/shard_map/ppermute | solution.py:259
  6.3 0.0 copy-start
  6.3 0.7 copy-done
  6.9 0.0 copy-start.2
  6.9 0.7 copy-done.2
  7.6 0.0 copy-start.3
  7.6 9.7 %shard_map.68 = (bf16[8,512,384]{2,1,0:T(8,128)(2,1)}, bf16[8,512,384]{2,1,0:T(8,128)(2,1)S(1)}, bf16[8,384,512]{2,1,0:T(8,128)(2,1)S(1)}, bf16[2,512,384]{2,1,0:T(8,128)(2,1)S(1)}) custom-call(s32[16]{0:T(128)S(1)} %collective-permute-done.above, s32[8]{0:T(128)S(1)} %copy-done, s32[1]{0:T(128)} %bitcast.me, s32[8]{0:T(128)S(1)} %copy-done.2, ...), custom_call_target="tpu_custom_call" | custom-call | flops 5637144576 | bytes 6815744 | tf_op jit(solution)/shard_map/pallas_call | solution.py:167
  17.3 0.0 copy-done.3
  17.3 0.0 copy-start.1
  17.4 10.0 %shard_map.69 = (bf16[8,512,384]{2,1,0:T(8,128)(2,1)}, bf16[8,512,384]{2,1,0:T(8,128)(2,1)S(1)}, bf16[8,384,512]{2,1,0:T(8,128)(2,1)S(1)}, bf16[2,512,384]{2,1,0:T(8,128)(2,1)S(1)}, bf16[4,512,384]{2,1,0:T(8,128)(2,1)S(1)}) custom-call(s32[16]{0:T(128)S(1)} %collective-permute-done.above, ...), custom_call_target="tpu_custom_call", output_to_operand_aliasing={{0}: (6, {}), {1}: (7, {}), {2}: (8, {})} | custom-call | flops 5637144576 | bytes 6815744 | tf_op jit(solution)/shard_map/pallas_call | solution.py:167
  27.4 1.9 %collective-permute-start.7 = (bf16[4,512,384]{2,1,0:T(8,128)(2,1)S(1)}, bf16[4,512,384]{2,1,0:T(8,128)(2,1)S(1)}, u32[]{:S(2)}, u32[]{:S(2)}) collective-permute-start(bf16[4,512,384]{2,1,0:T(8,128)(2,1)S(1)} %get-tuple-element.31), channel_id=1, source_target_pairs={{0,8},{8,16},{16,24},{1,9},{9,17},{17,25},{2,10},{10,18},{18,26},{... | collective-permute-start | bytes 4718600 | tf_op jit(solution)/shard_map/ppermute | solution.py:265
  29.3 1.9 %collective-permute-start.1 = (bf16[2,512,384]{2,1,0:T(8,128)(2,1)S(1)}, bf16[2,512,384]{2,1,0:T(8,128)(2,1)S(1)}, u32[]{:S(2)}, u32[]{:S(2)}) collective-permute-start(bf16[2,512,384]{2,1,0:T(8,128)(2,1)S(1)} %get-tuple-element.25), channel_id=1, source_target_pairs={{0,8},{8,16},{16,24},{1,9},{9,17},{17,25},{2,10},{10,18},{18,26},{... | collective-permute-start | bytes 2359304 | tf_op jit(solution)/shard_map/ppermute | solution.py:265
  31.3 1.9 %collective-permute-start.4 = (bf16[2,512,384]{2,1,0:T(8,128)(2,1)S(1)}, bf16[2,512,384]{2,1,0:T(8,128)(2,1)S(1)}, u32[]{:S(2)}, u32[]{:S(2)}) collective-permute-start(bf16[2,512,384]{2,1,0:T(8,128)(2,1)S(1)} %get-tuple-element.28), channel_id=1, source_target_pairs={{0,8},{8,16},{16,24},{1,9},{9,17},{17,25},{2,10},{10,18},{18,26},{... | collective-permute-start | bytes 2359304 | tf_op jit(solution)/shard_map/ppermute | solution.py:265
  33.2 21.9 %collective-permute-done.1.low_ref = bf16[2,512,384]{2,1,0:T(8,128)(2,1)S(1)} collective-permute-done((bf16[2,512,384]{2,1,0:T(8,128)(2,1)S(1)}, bf16[2,512,384]{2,1,0:T(8,128)(2,1)S(1)}, u32[]{:S(2)}, u32[]{:S(2)}) %collective-permute-start.1) | collective-permute-done | bytes 786464 | tf_op jit(solution)/shard_map/ppermute | solution.py:265
  55.1 0.0 copy-done.1
  55.1 1.5 %shard_map.70 = (bf16[1,384,384]{2,1,0:T(8,128)(2,1)S(1)}, bf16[1,384,384]{2,1,0:T(8,128)(2,1)S(1)}) custom-call(s32[8]{0:T(128)S(1)} %copy-done.1, s32[1]{0:T(128)} %bitcast.me, bf16[8,512,384]{2,1,0:T(8,128)(2,1)S(1)} %get-tuple-element.23.x_ref, bf16[8,384,512]{2,1,0:T(8,128)(2,1)S(1)} %get-tuple-element.24.y_ref, ...), custom_call_target="tpu_custom_call" | custom-call | flops 603979776 | bytes 2949120 | tf_op jit(solution)/shard_map/pallas_call | solution.py:207
  56.6 0.6 collective-permute-start.2
  57.3 0.6 collective-permute-start.3
  57.9 5.6 %collective-permute-done.4.low_ref = bf16[2,512,384]{2,1,0:T(8,128)(2,1)S(1)} collective-permute-done((bf16[2,512,384]{2,1,0:T(8,128)(2,1)S(1)}, bf16[2,512,384]{2,1,0:T(8,128)(2,1)S(1)}, u32[]{:S(2)}, u32[]{:S(2)}) %collective-permute-start.4) | collective-permute-done | bytes 786464 | tf_op jit(solution)/shard_map/ppermute | solution.py:265
  63.5 1.5 %shard_map.71 = (bf16[1,384,384]{2,1,0:T(8,128)(2,1)S(1)}, bf16[1,384,384]{2,1,0:T(8,128)(2,1)S(1)}) custom-call(s32[8]{0:T(128)S(1)} %copy-done.1, s32[1]{0:T(128)} %bitcast.me, bf16[8,512,384]{2,1,0:T(8,128)(2,1)S(1)} %get-tuple-element.23.x_ref, bf16[8,384,512]{2,1,0:T(8,128)(2,1)S(1)} %get-tuple-element.24.y_ref, ...), custom_call_target="tpu_custom_call" | custom-call | flops 603979776 | bytes 2949120 | tf_op jit(solution)/shard_map/pallas_call | solution.py:207
  65.0 0.1 collective-permute-start.5
  65.1 0.7 collective-permute-start.6
  65.8 0.0 collective-permute-done.7.low_ref
  65.8 2.3 %shard_map.72 = (bf16[1,384,384]{2,1,0:T(8,128)(2,1)S(1)}, bf16[1,384,384]{2,1,0:T(8,128)(2,1)S(1)}, bf16[1,384,384]{2,1,0:T(8,128)(2,1)S(1)}, bf16[1,384,384]{2,1,0:T(8,128)(2,1)S(1)}) custom-call(s32[8]{0:T(128)S(1)} %copy-done.1, s32[1]{0:T(128)} %bitcast.me, bf16[8,512,384]{2,1,0:T(8,128)(2,1)S(1)} %get-tuple-element.23.x_ref, ...), custom_call_target="tpu_custom_call" | custom-call | flops 1207959552 | bytes 5898240 | tf_op jit(solution)/shard_map/pallas_call | solution.py:207
  68.2 3.2 %collective-permute-start.8 = (bf16[1,384,384]{2,1,0:T(8,128)(2,1)S(1)}, bf16[1,384,384]{2,1,0:T(8,128)(2,1)S(1)}, u32[]{:S(2)}, u32[]{:S(2)}) collective-permute-start(bf16[1,384,384]{2,1,0:T(8,128)(2,1)S(1)} %get-tuple-element.32), channel_id=1, source_target_pairs={{0,3},{1,2},{2,1},{3,0},{4,7},{5,6},{6,5},{7,4},{8,11},{9,10},{10,... | collective-permute-start | bytes 884744 | tf_op jit(solution)/shard_map/ppermute | solution.py:271
  71.4 5.3 %collective-permute-done.2.refs_0_ = bf16[1,384,384]{2,1,0:T(8,128)(2,1)S(1)} collective-permute-done((bf16[1,384,384]{2,1,0:T(8,128)(2,1)S(1)}, bf16[1,384,384]{2,1,0:T(8,128)(2,1)S(1)}, u32[]{:S(2)}, u32[]{:S(2)}) %collective-permute-start.2) | collective-permute-done | bytes 294944 | tf_op jit(solution)/shard_map/ppermute | solution.py:271
  76.7 2.0 %collective-permute-start.9 = (bf16[1,384,384]{2,1,0:T(8,128)(2,1)S(1)}, bf16[1,384,384]{2,1,0:T(8,128)(2,1)S(1)}, u32[]{:S(2)}, u32[]{:S(2)}) collective-permute-start(bf16[1,384,384]{2,1,0:T(8,128)(2,1)S(1)} %get-tuple-element.33), channel_id=1, source_target_pairs={{0,2},{1,3},{2,0},{3,1},{4,6},{5,7},{6,4},{7,5},{8,10},{9,11},{10,... | collective-permute-start | bytes 884744 | tf_op jit(solution)/shard_map/ppermute | solution.py:271
  78.7 2.5 %collective-permute-done.3.refs_1_ = bf16[1,384,384]{2,1,0:T(8,128)(2,1)S(1)} collective-permute-done((bf16[1,384,384]{2,1,0:T(8,128)(2,1)S(1)}, bf16[1,384,384]{2,1,0:T(8,128)(2,1)S(1)}, u32[]{:S(2)}, u32[]{:S(2)}) %collective-permute-start.3) | collective-permute-done | bytes 294944 | tf_op jit(solution)/shard_map/ppermute | solution.py:271
  81.2 0.8 collective-permute-start.10
  82.0 3.3 %collective-permute-done.5.refs_2_ = bf16[1,384,384]{2,1,0:T(8,128)(2,1)S(1)} collective-permute-done((bf16[1,384,384]{2,1,0:T(8,128)(2,1)S(1)}, bf16[1,384,384]{2,1,0:T(8,128)(2,1)S(1)}, u32[]{:S(2)}, u32[]{:S(2)}) %collective-permute-start.5) | collective-permute-done | bytes 294944 | tf_op jit(solution)/shard_map/ppermute | solution.py:271
  85.3 3.1 %collective-permute-done.6.refs_3_ = bf16[1,384,384]{2,1,0:T(8,128)(2,1)S(1)} collective-permute-done((bf16[1,384,384]{2,1,0:T(8,128)(2,1)S(1)}, bf16[1,384,384]{2,1,0:T(8,128)(2,1)S(1)}, u32[]{:S(2)}, u32[]{:S(2)}) %collective-permute-start.6) | collective-permute-done | bytes 294944 | tf_op jit(solution)/shard_map/ppermute | solution.py:271
  88.4 0.0 collective-permute-done.8.refs_4_
  88.4 0.0 collective-permute-done.9.refs_5_
  88.4 1.5 %collective-permute-done.10.refs_6_ = bf16[1,384,384]{2,1,0:T(8,128)(2,1)S(1)} collective-permute-done((bf16[1,384,384]{2,1,0:T(8,128)(2,1)S(1)}, bf16[1,384,384]{2,1,0:T(8,128)(2,1)S(1)}, u32[]{:S(2)}, u32[]{:S(2)}) %collective-permute-start.10) | collective-permute-done | bytes 294944 | tf_op jit(solution)/shard_map/ppermute | solution.py:271
  89.9 1.5 %shard_map.73 = bf16[8,384,384]{2,1,0:T(8,128)(2,1)} custom-call(s32[1]{0:T(128)} %bitcast.me, bf16[1,384,384]{2,1,0:T(8,128)(2,1)S(1)} %collective-permute-done.2.refs_0_, bf16[1,384,384]{2,1,0:T(8,128)(2,1)S(1)} %collective-permute-done.3.refs_1_, bf16[1,384,384]{2,1,0:T(8,128)(2,1)S(1)} %collective-permute-done.5.refs_2_, ...), custom_call_target="tpu_custom_call" | custom-call | bytes 4718592 | tf_op jit(solution)/shard_map/pallas_call | solution.py:236
Async XLA Ops:
  1.4 4.9 %collective-permute-start = (s32[16]{0:T(128)S(1)}, s32[16]{0:T(128)S(1)}, u32[]{:S(2)}, u32[]{:S(2)}) collective-permute-start(s32[16]{0:T(128)S(1)} %pad_add_fusion), channel_id=1, source_target_pairs={{8,0},{16,8},{24,16},{9,1},{17,9},{25,17},{10,2},{18,10},{26,18},{... | collective-permute-start | bytes 200 | tf_op jit(solution)/shard_map/ppermute | solution.py:259
  6.3 0.7 copy-start
  6.9 0.7 copy-start.2
  7.6 9.7 %copy-start.3 = (s32[8]{0:T(128)S(1)}, s32[8]{0:T(128)}, u32[]{:S(2)}) copy-start(s32[8]{0:T(128)} %counts.3) | copy-start | bytes 100
  17.3 37.8 %copy-start.1 = (s32[8]{0:T(128)S(1)}, s32[8]{0:T(128)}, u32[]{:S(2)}) copy-start(s32[8]{0:T(128)} %task.9) | copy-start | bytes 100
  27.4 38.4 %collective-permute-start.7 = (bf16[4,512,384]{2,1,0:T(8,128)(2,1)S(1)}, bf16[4,512,384]{2,1,0:T(8,128)(2,1)S(1)}, u32[]{:S(2)}, u32[]{:S(2)}) collective-permute-start(bf16[4,512,384]{2,1,0:T(8,128)(2,1)S(1)} %get-tuple-element.31), channel_id=1, source_target_pairs={{0,8},{8,16},{16,24},{1,9},{9,17},{17,25},{2,10},{10,18},{18,26},{... | collective-permute-start | bytes 4718600 | tf_op jit(solution)/shard_map/ppermute | solution.py:265
  29.3 25.8 %collective-permute-start.1 = (bf16[2,512,384]{2,1,0:T(8,128)(2,1)S(1)}, bf16[2,512,384]{2,1,0:T(8,128)(2,1)S(1)}, u32[]{:S(2)}, u32[]{:S(2)}) collective-permute-start(bf16[2,512,384]{2,1,0:T(8,128)(2,1)S(1)} %get-tuple-element.25), channel_id=1, source_target_pairs={{0,8},{8,16},{16,24},{1,9},{9,17},{17,25},{2,10},{10,18},{18,26},{... | collective-permute-start | bytes 2359304 | tf_op jit(solution)/shard_map/ppermute | solution.py:265
  31.3 32.3 %collective-permute-start.4 = (bf16[2,512,384]{2,1,0:T(8,128)(2,1)S(1)}, bf16[2,512,384]{2,1,0:T(8,128)(2,1)S(1)}, u32[]{:S(2)}, u32[]{:S(2)}) collective-permute-start(bf16[2,512,384]{2,1,0:T(8,128)(2,1)S(1)} %get-tuple-element.28), channel_id=1, source_target_pairs={{0,8},{8,16},{16,24},{1,9},{9,17},{17,25},{2,10},{10,18},{18,26},{... | collective-permute-start | bytes 2359304 | tf_op jit(solution)/shard_map/ppermute | solution.py:265
  56.6 20.1 %collective-permute-start.2 = (bf16[1,384,384]{2,1,0:T(8,128)(2,1)S(1)}, bf16[1,384,384]{2,1,0:T(8,128)(2,1)S(1)}, u32[]{:S(2)}, u32[]{:S(2)}) collective-permute-start(bf16[1,384,384]{2,1,0:T(8,128)(2,1)S(1)} %get-tuple-element.26), channel_id=1, source_target_pairs={{0,4},{1,5},{2,6},{3,7},{4,0},{5,1},{6,2},{7,3},{8,12},{9,13},{10,... | collective-permute-start | bytes 884744 | tf_op jit(solution)/shard_map/ppermute | solution.py:271
  57.3 23.9 %collective-permute-start.3 = (bf16[1,384,384]{2,1,0:T(8,128)(2,1)S(1)}, bf16[1,384,384]{2,1,0:T(8,128)(2,1)S(1)}, u32[]{:S(2)}, u32[]{:S(2)}) collective-permute-start(bf16[1,384,384]{2,1,0:T(8,128)(2,1)S(1)} %get-tuple-element.27), channel_id=1, source_target_pairs={{0,5},{1,4},{2,7},{3,6},{4,1},{5,0},{6,3},{7,2},{8,13},{9,12},{10,... | collective-permute-start | bytes 884744 | tf_op jit(solution)/shard_map/ppermute | solution.py:271
  65.0 20.3 %collective-permute-start.5 = (bf16[1,384,384]{2,1,0:T(8,128)(2,1)S(1)}, bf16[1,384,384]{2,1,0:T(8,128)(2,1)S(1)}, u32[]{:S(2)}, u32[]{:S(2)}) collective-permute-start(bf16[1,384,384]{2,1,0:T(8,128)(2,1)S(1)} %get-tuple-element.29), channel_id=1, source_target_pairs={{0,6},{1,7},{2,4},{3,5},{4,2},{5,3},{6,0},{7,1},{8,14},{9,15},{10,... | collective-permute-start | bytes 884744 | tf_op jit(solution)/shard_map/ppermute | solution.py:271
  65.1 23.3 %collective-permute-start.6 = (bf16[1,384,384]{2,1,0:T(8,128)(2,1)S(1)}, bf16[1,384,384]{2,1,0:T(8,128)(2,1)S(1)}, u32[]{:S(2)}, u32[]{:S(2)}) collective-permute-start(bf16[1,384,384]{2,1,0:T(8,128)(2,1)S(1)} %get-tuple-element.30), channel_id=1, source_target_pairs={{0,7},{1,6},{2,5},{3,4},{4,3},{5,2},{6,1},{7,0},{8,15},{9,14},{10,... | collective-permute-start | bytes 884744 | tf_op jit(solution)/shard_map/ppermute | solution.py:271
  68.2 20.3 %collective-permute-start.8 = (bf16[1,384,384]{2,1,0:T(8,128)(2,1)S(1)}, bf16[1,384,384]{2,1,0:T(8,128)(2,1)S(1)}, u32[]{:S(2)}, u32[]{:S(2)}) collective-permute-start(bf16[1,384,384]{2,1,0:T(8,128)(2,1)S(1)} %get-tuple-element.32), channel_id=1, source_target_pairs={{0,3},{1,2},{2,1},{3,0},{4,7},{5,6},{6,5},{7,4},{8,11},{9,10},{10,... | collective-permute-start | bytes 884744 | tf_op jit(solution)/shard_map/ppermute | solution.py:271
  76.7 11.7 %collective-permute-start.9 = (bf16[1,384,384]{2,1,0:T(8,128)(2,1)S(1)}, bf16[1,384,384]{2,1,0:T(8,128)(2,1)S(1)}, u32[]{:S(2)}, u32[]{:S(2)}) collective-permute-start(bf16[1,384,384]{2,1,0:T(8,128)(2,1)S(1)} %get-tuple-element.33), channel_id=1, source_target_pairs={{0,2},{1,3},{2,0},{3,1},{4,6},{5,7},{6,4},{7,5},{8,10},{9,11},{10,... | collective-permute-start | bytes 884744 | tf_op jit(solution)/shard_map/ppermute | solution.py:271
  81.2 8.7 %collective-permute-start.10 = (bf16[1,384,384]{2,1,0:T(8,128)(2,1)S(1)}, bf16[1,384,384]{2,1,0:T(8,128)(2,1)S(1)}, u32[]{:S(2)}, u32[]{:S(2)}) collective-permute-start(bf16[1,384,384]{2,1,0:T(8,128)(2,1)S(1)} %get-tuple-element.34), channel_id=1, source_target_pairs={{0,1},{1,0},{2,3},{3,2},{4,5},{5,4},{6,7},{7,6},{8,9},{9,8},{10,11... | collective-permute-start | bytes 884744 | tf_op jit(solution)/shard_map/ppermute | solution.py:271

commit v2 on v1

--- a/solution.py
+++ b/solution.py
@@ -53,40 +53,60 @@
         return found
 
 
-def arrange(route, early, above, task, me, order):
+def load_kernel(a_hbm, b_hbm, a_ref, b_ref, sems):
+    copies = []
+    for g in range(a_hbm.shape[0]):
+        copies.append(pltpu.make_async_copy(a_hbm.at[g], a_ref.at[g], sems.at[0, g]))
+        copies.append(pltpu.make_async_copy(b_hbm.at[g], b_ref.at[g], sems.at[1, g]))
+    for copy in copies:
+        copy.start()
+    for copy in copies:
+        copy.wait()
+
+
+def load(matrices, basis):
+    return pl.pallas_call(
+        load_kernel,
+        in_specs=[ANY] * 2,
+        out_specs=[VMEM] * 2,
+        out_shape=[pltpu.VMEM(a.shape, a.dtype) for a in (matrices, basis)],
+        scratch_shapes=[pltpu.SemaphoreType.DMA((2, matrices.shape[0]))],
+        compiler_params=limit(8),
+        cost_estimate=pl.CostEstimate(
+            flops=0, bytes_accessed=2 * (matrices.size + basis.size), transcendentals=0
+        ),
+    )(in_hbm(matrices), in_hbm(basis))
+
+
+def arrange(route, local, above, me, order, seen):
     columns = route.columns
-    needed = [route.slot(task, me[0], j) for j in range(early)]
-    needed += [above[columns + route.slot(above, me[0], j)] for j in range(early)]
-    first = [
-        functools.reduce(jnp.maximum, [(n == s).astype(jnp.int32) for n in needed])
-        for s in range(columns)
-    ]
-    ahead, behind = jnp.int32(0), functools.reduce(jnp.add, first)
     for s in range(columns):
-        order[jnp.where(first[s] > 0, ahead, behind)] = s
-        ahead, behind = ahead + first[s], behind + 1 - first[s]
-
-
-def smooth_kernel(route, early, begin, n, cuts, above, task, me, counts, a_hbm, b_hbm, *refs):
+        seen[s] = 0
+    listed = []
+    for j in range(2):
+        listed.append(route.slot(local, me[0], j))
+        listed.append(above[columns + route.slot(above, me[0], j)])
+    count = jnp.int32(0)
+    for s in listed + list(range(columns)):
+        fresh = 1 - seen[s]
+
+        @pl.when(fresh == 1)
+        def _():
+            order[count] = s
+
+        seen[s] = 1
+        count = count + fresh
+
+
+def smooth_kernel(route, begin, n, cuts, waits, local, above, me, a_ref, b_ref, *refs):
     chunks = len(cuts) - 1
-    refs = refs[3:] if begin else refs
+    refs = refs[3 + waits :] if begin else refs
     x_ref, xv_ref, y_ref = refs[:3]
     sent = refs[3 : 3 + chunks]
-    order, a_buf, b_buf, in_sems, out_sems, sent_sems = refs[3 + chunks :]
-    width, modes = b_buf.shape[1:]
+    order, seen, out_sems, sent_sems = refs[3 + chunks :]
+    width, modes = b_ref.shape[1:]
     columns = route.columns
-    arrange(route, early, above, task, me, order)
-
-    def loads(p):
-        g = order[begin + p]
-        return (
-            pltpu.make_async_copy(a_hbm.at[g], a_buf.at[p], in_sems.at[0, p]),
-            pltpu.make_async_copy(b_hbm.at[g], b_buf.at[p], in_sems.at[1, p]),
-        )
-
-    for p in range(n):
-        for copy in loads(p):
-            copy.start()
+    arrange(route, local, above, me, order, seen)
 
     wanted, emits = [], []
     for out, a, b in zip(sent, cuts[:-1], cuts[1:]):
@@ -112,10 +132,7 @@
     def _(i):
         at = [2 * i, 2 * i + 1]
         slots = [order[begin + p] for p in at]
-        for p in at:
-            for copy in loads(p):
-                copy.wait()
-        mine = [counts[g] for g in slots]
+        mine = [local[2 * columns + g] for g in slots]
         groups = pl.cdiv(jnp.maximum(*mine), TILE)
         for live in range(1, modes // TILE + 1):
 
@@ -125,20 +142,20 @@
                 rows = lax.broadcasted_iota(jnp.int32, (top, width), 0)
                 zero = jnp.zeros((), jnp.bfloat16)
                 current = [
-                    jnp.where(rows < count, b_buf[p, :, :top].T, zero)
-                    for p, count in zip(at, mine)
+                    jnp.where(rows < count, b_ref[g, :, :top].T, zero)
+                    for g, count in zip(slots, mine)
                 ]
                 for weight in omegas:
                     product = [
-                        jnp.dot(c, a_buf[p], preferred_element_type=jnp.float32)
-                        for p, c in zip(at, current)
+                        jnp.dot(c, a_ref[g], preferred_element_type=jnp.float32)
+                        for g, c in zip(slots, current)
                     ]
                     current = [
                         (c.astype(jnp.float32) - weight * d).astype(jnp.bfloat16)
                         for c, d in zip(current, product)
                     ]
-                for p, g, c in zip(at, slots, current):
-                    image = jnp.dot(c, a_buf[p], preferred_element_type=jnp.float32)
+                for g, c in zip(slots, current):
+                    image = jnp.dot(c, a_ref[g], preferred_element_type=jnp.float32)
                     y_ref[g, :top, :] = image.astype(jnp.bfloat16)
                     xv_ref[g, :, :top] = c.T
                     if top < modes:
@@ -159,20 +176,21 @@
         emit.wait()
 
 
-def smooth(route, early, begin, n, cuts, above, task, me, counts, matrices, basis, before):
+def smooth(route, begin, n, cuts, local, above, me, matrices, basis, before, after=()):
     total, width, modes = basis.shape
     spans = [b - a for a, b in zip(cuts[:-1], cuts[1:])]
     if before:
         before = [before[0], in_vmem(before[1]), in_vmem(before[2])]
     return pl.pallas_call(
-        functools.partial(smooth_kernel, route, early, begin, n, cuts),
-        in_specs=[SMEM] * 4 + [ANY] * 2 + ([ANY, VMEM, VMEM] if before else []),
+        functools.partial(smooth_kernel, route, begin, n, cuts, len(after)),
+        in_specs=[SMEM] * 3
+        + [VMEM] * 2
+        + ([ANY, VMEM, VMEM] if before else [])
+        + [ANY] * len(after),
         out_specs=[ANY, VMEM, VMEM] + [ANY] * len(spans),
         scratch_shapes=[
             pltpu.SMEM((total,), jnp.int32),
-            pltpu.VMEM((n, width, width), jnp.bfloat16),
-            pltpu.VMEM((n, width, modes), jnp.bfloat16),
-            pltpu.SemaphoreType.DMA((2, n)),
+            pltpu.SMEM((total,), jnp.int32),
             pltpu.SemaphoreType.DMA((n,)),
             pltpu.SemaphoreType.DMA((cuts[-1] - cuts[0],)),
         ],
@@ -182,14 +200,14 @@
             pltpu.VMEM((total, modes, width), jnp.bfloat16),
         ]
         + [jax.ShapeDtypeStruct((m, width, modes), jnp.bfloat16) for m in spans],
-        input_output_aliases={6: 0, 7: 1, 8: 2} if before else {},
-        compiler_params=limit(24),
+        input_output_aliases={5: 0, 6: 1, 7: 2} if before else {},
+        compiler_params=limit(16),
         cost_estimate=pl.CostEstimate(
             flops=14 * n * width * width * modes,
             bytes_accessed=2 * n * width * (width + 3 * modes),
             transcendentals=0,
         ),
-    )(above, task, me, counts, in_hbm(matrices), in_hbm(basis), *before)
+    )(local, above, me, in_vmem(matrices), in_vmem(basis), *before, *after)
 
 
 def block_kernel(route, begin, task, me, x_ref, y_ref, low_ref, *outs):
@@ -252,25 +270,39 @@
     me = lax.axis_index("ay").astype(jnp.int32).reshape(1)
     down = [(i + 1, i) for i in range(rows - 1)]
     up = [(i, i + 1) for i in range(rows - 1)]
-    early = columns // 4
-    cuts = (0, early, 2 * early, columns)
-    half = columns // 2
-
-    above = lax.ppermute(jnp.concatenate([task_map, neighbour]), "ax", down)
-    scalars = (above, task_map, me, mode_counts, matrices, basis_cols)
-    *kept, first = smooth(route, early, 0, half, cuts[:2], *scalars, [])
-    out, x, y, *others = smooth(route, early, half, half, cuts[1:], *scalars, kept)
-    lows = []
-    for chosen in [first, *others]:
-        lows.append(lax.ppermute(chosen, "ax", up))
-    arrived = []
-    for a, b, low in zip(cuts[:-1], cuts[1:], lows):
-        made = blocks(route, a, b - a, task_map, me, x, y, low)
-        for j, block in zip(range(a, b), made):
-            if route.steps[j]:
-                block = lax.ppermute(block, "ay", route.pairs(route.steps[j]))
-            arrived.append(block)
-    return out, place(route, me, arrived)
+    cuts = (0, 1, 2, columns // 2, columns)
+    spans = list(zip(cuts[:-1], cuts[1:]))
+
+    local = jnp.concatenate([task_map, neighbour, mode_counts])
+    above = lax.ppermute(local, "ax", down)
+    loaded = load(matrices, basis_cols)
+    scalars = (local, above, me, *loaded)
+
+    def fetch(chosen):
+        return lax.ppermute(chosen, "ax", up)
+
+    def exchange(j, x, y, low):
+        a, b = spans[j]
+        made = blocks(route, a, b - a, local, me, x, y, low)
+        pieces = []
+        for i, block in zip(range(a, b), made):
+            if route.steps[i]:
+                block = lax.ppermute(block, "ay", route.pairs(route.steps[i]))
+            pieces.append(block)
+        return made, pieces
+
+    *kept, chosen = smooth(route, 0, 2, cuts[:2], *scalars, [])
+    low0 = fetch(chosen)
+    *kept, chosen = smooth(route, 2, 2, cuts[1:3], *scalars, kept)
+    low1 = fetch(chosen)
+    made0, pieces0 = exchange(0, kept[1], kept[2], low0)
+    made1, pieces1 = exchange(1, kept[1], kept[2], low1)
+    out, x, y, chosen2, chosen3 = smooth(
+        route, 4, columns - 4, cuts[2:], *scalars, kept, [made0[0], made1[0]]
+    )
+    low2, low3 = fetch(chosen2), fetch(chosen3)
+    pieces = pieces0 + pieces1 + exchange(2, x, y, low2)[1] + exchange(3, x, y, low3)[1]
+    return out, place(route, me, pieces)
 
 
 def solution(mesh):

time: 91.8 us -> 102 us (1.11)
  starting transfers between devices: 16.4 us -> 26.4 us
  Pallas kernels: 26.6 us -> 28.8 us
  local copies, waits for them, and re-layouts: 1.32 us -> 0 us
    ppermute x11 -> x12, starting transfers between devices: 16.4 us -> 26.4 us  [the longest x7 12.9 us: exchange(): block = lax.ppermute(block, 'ay', route.pairs(route.steps[i]))]
    pallas_call x2 -> x4, Pallas kernels: 19.8 us -> 21.2 us  [the longest x3 18 us: smooth(): pl.pallas_call(functools.partial(smooth_kernel, route, begin, n, cuts, le...]
    unnamed x8 -> x0, local copies, waits for them, and re-layouts: 1.32 us -> none
    pallas_call x3 -> x4, Pallas kernels: 5.37 us -> 6.11 us  [blocks(): pl.pallas_call(functools.partial(block_kernel, route, begin), in_specs=[S...]
    ppermute x11 -> x12, waiting for transfers between devices: 45.6 us -> 45.3 us  [the longest x4 24.1 us: fetch(): return lax.ppermute(chosen, 'ax', up)]
  transfers between devices with their start and end apart: 11 -> 12, of which waited for: 8 -> 6; matrix products, arithmetic and copies ran while one was open for 0% -> 0% of each run, Pallas kernels for 6% -> 8%
where the time goes in v2:
time: 102 us
  waiting for transfers between devices  45.3 us (44%)
  Pallas kernels  28.8 us (28%)
  starting transfers between devices  26.4 us (26%)
    ppermute x4, waiting for transfers between devices, fetch(): return lax.ppermute(chosen, 'ax', up)  24.1 us
    ppermute x7, waiting for transfers between devices, exchange(): block = lax.ppermute(block, 'ay', route.pairs(route.steps[i]))  21.2 us
    pallas_call x3, Pallas kernels, smooth(): pl.pallas_call(functools.partial(smooth_kernel, route, begin, n, cuts, le...  18 us
    ppermute x7, starting transfers between devices, exchange(): block = lax.ppermute(block, 'ay', route.pairs(route.steps[i]))  12.9 us
    ppermute x4, starting transfers between devices, fetch(): return lax.ppermute(chosen, 'ax', up)  10.8 us
    pallas_call x4, Pallas kernels, blocks(): pl.pallas_call(functools.partial(block_kernel, route, begin), in_specs=[S...  6.11 us
    pallas_call x1, Pallas kernels, load(): pl.pallas_call(load_kernel, in_specs=[ANY] * 2, out_specs=[VMEM] * 2, out...  3.21 us
    ppermute x1, starting transfers between devices, body(): above = lax.ppermute(local, 'ax', down)  2.57 us
  transfers between devices with their start and end apart: 12, of which 6 were waited for; matrix products, arithmetic and copies ran while one was open for 0% of the time, Pallas kernels for 8%

profile of v2, /device:TPU:9, one launch (start us, length us, event | category | flops | bytes accessed | tf_op | source)
XLA Modules:
  0.0 102.2 jit_solution(12996296169986590996)
XLA Ops:
  0.6 0.8 pad_add_fusion.local.task
  1.4 2.6 %collective-permute-start = (s32[24]{0:T(128)S(1)}, s32[24]{0:T(128)S(1)}, u32[]{:S(2)}, u32[]{:S(2)}) collective-permute-start(s32[24]{0:T(128)S(1)} %pad_add_fusion.local.task), channel_id=1, source_target_pairs={{8,0},{16,8},{24,16},{9,1},{17,9},{25,17},{10,2},{18,10},{26,18},{... | collective-permute-start | bytes 296 | tf_op jit(solution)/shard_map/ppermute | solution.py:277
  4.0 3.2 %shard_map.68 = (bf16[8,512,512]{2,1,0:T(8,128)(2,1)S(1)}, bf16[8,512,384]{2,1,0:T(8,128)(2,1)S(1)}) custom-call(bf16[8,512,512]{2,1,0:T(8,128)(2,1)} %a_hbm.1, bf16[8,512,384]{2,1,0:T(8,128)(2,1)} %b_hbm.1), custom_call_target="tpu_custom_call" | custom-call | bytes 7340032 | tf_op jit(solution)/shard_map/pallas_call | solution.py:68
  7.2 0.0 collective-permute-done.above
  7.2 4.7 %shard_map.69 = (bf16[8,512,384]{2,1,0:T(8,128)(2,1)}, bf16[8,512,384]{2,1,0:T(8,128)(2,1)S(1)}, bf16[8,384,512]{2,1,0:T(8,128)(2,1)S(1)}, bf16[1,512,384]{2,1,0:T(8,128)(2,1)S(1)}) custom-call(s32[24]{0:T(128)S(1)} %pad_add_fusion.local.task, s32[24]{0:T(128)S(1)} %collective-permute-done.above, s32[1]{0:T(128)} %bitcast.me, ...), custom_call_target="tpu_custom_call" | custom-call | flops 2818572288 | bytes 3407872 | tf_op jit(solution)/shard_map/pallas_call | solution.py:184
  11.9 4.7 %shard_map.70 = (bf16[8,512,384]{2,1,0:T(8,128)(2,1)}, bf16[8,512,384]{2,1,0:T(8,128)(2,1)S(1)}, bf16[8,384,512]{2,1,0:T(8,128)(2,1)S(1)}, bf16[1,512,384]{2,1,0:T(8,128)(2,1)S(1)}) custom-call(s32[24]{0:T(128)S(1)} %pad_add_fusion.local.task, s32[24]{0:T(128)S(1)} %collective-permute-done.above, ...), custom_call_target="tpu_custom_call", output_to_operand_aliasing={{0}: (5, {}), {1}: (6, {}), {2}: (7, {})} | custom-call | flops 2818572288 | bytes 3407872 | tf_op jit(solution)/shard_map/pallas_call | solution.py:184
  16.6 2.1 %collective-permute-start.2 = (bf16[1,512,384]{2,1,0:T(8,128)(2,1)S(1)}, bf16[1,512,384]{2,1,0:T(8,128)(2,1)S(1)}, u32[]{:S(2)}, u32[]{:S(2)}) collective-permute-start(bf16[1,512,384]{2,1,0:T(8,128)(2,1)S(1)} %get-tuple-element.32), channel_id=1, source_target_pairs={{0,8},{8,16},{16,24},{1,9},{9,17},{17,25},{2,10},{10,18},{18,26},{... | collective-permute-start | bytes 1179656 | tf_op jit(solution)/shard_map/ppermute | solution.py:282
  18.7 3.7 %collective-permute-start.1 = (bf16[1,512,384]{2,1,0:T(8,128)(2,1)S(1)}, bf16[1,512,384]{2,1,0:T(8,128)(2,1)S(1)}, u32[]{:S(2)}, u32[]{:S(2)}) collective-permute-start(bf16[1,512,384]{2,1,0:T(8,128)(2,1)S(1)} %get-tuple-element.31), channel_id=1, source_target_pairs={{0,8},{8,16},{16,24},{1,9},{9,17},{17,25},{2,10},{10,18},{18,26},{... | collective-permute-start | bytes 1179656 | tf_op jit(solution)/shard_map/ppermute | solution.py:282
  22.4 1.0 collective-permute-done.2.low_ref
  23.4 1.1 %shard_map.72.refs_4_ = bf16[1,384,384]{2,1,0:T(8,128)(2,1)S(1)} custom-call(s32[24]{0:T(128)S(1)} %pad_add_fusion.local.task, s32[1]{0:T(128)} %bitcast.me, bf16[8,512,384]{2,1,0:T(8,128)(2,1)S(1)} %get-tuple-element.29.x_ref.refs_1_, bf16[8,384,512]{2,1,0:T(8,128)(2,1)S(1)} %get-tuple-element.30.y_ref.refs_2_, ...), custom_call_target="tpu_custom_call" | custom-call | flops 301989888 | bytes 1474560 | tf_op jit(solution)/shard_map/pallas_call | solution.py:225
  24.5 3.1 %collective-permute-done.1.low_ref = bf16[1,512,384]{2,1,0:T(8,128)(2,1)S(1)} collective-permute-done((bf16[1,512,384]{2,1,0:T(8,128)(2,1)S(1)}, bf16[1,512,384]{2,1,0:T(8,128)(2,1)S(1)}, u32[]{:S(2)}, u32[]{:S(2)}) %collective-permute-start.1) | collective-permute-done | bytes 393248 | tf_op jit(solution)/shard_map/ppermute | solution.py:282
  27.6 1.1 %shard_map.71.refs_3_ = bf16[1,384,384]{2,1,0:T(8,128)(2,1)S(1)} custom-call(s32[24]{0:T(128)S(1)} %pad_add_fusion.local.task, s32[1]{0:T(128)} %bitcast.me, bf16[8,512,384]{2,1,0:T(8,128)(2,1)S(1)} %get-tuple-element.29.x_ref.refs_1_, bf16[8,384,512]{2,1,0:T(8,128)(2,1)S(1)} %get-tuple-element.30.y_ref.refs_2_, ...), custom_call_target="tpu_custom_call" | custom-call | flops 301989888 | bytes 1474560 | tf_op jit(solution)/shard_map/pallas_call | solution.py:225
  28.8 8.7 %shard_map.73 = (bf16[8,512,384]{2,1,0:T(8,128)(2,1)}, bf16[8,512,384]{2,1,0:T(8,128)(2,1)S(1)}, bf16[8,384,512]{2,1,0:T(8,128)(2,1)S(1)}, bf16[2,512,384]{2,1,0:T(8,128)(2,1)S(1)}, bf16[4,512,384]{2,1,0:T(8,128)(2,1)S(1)}) custom-call(s32[24]{0:T(128)S(1)} %pad_add_fusion.local.task, ...), custom_call_target="tpu_custom_call", output_to_operand_aliasing={{0}: (5, {}), {1}: (6, {}), {2}: (7, {})} | custom-call | flops 5637144576 | bytes 6815744 | tf_op jit(solution)/shard_map/pallas_call | solution.py:184
  37.4 3.1 %collective-permute-start.8 = (bf16[4,512,384]{2,1,0:T(8,128)(2,1)S(1)}, bf16[4,512,384]{2,1,0:T(8,128)(2,1)S(1)}, u32[]{:S(2)}, u32[]{:S(2)}) collective-permute-start(bf16[4,512,384]{2,1,0:T(8,128)(2,1)S(1)} %get-tuple-element.39), channel_id=1, source_target_pairs={{0,8},{8,16},{16,24},{1,9},{9,17},{17,25},{2,10},{10,18},{18,26},{... | collective-permute-start | bytes 4718600 | tf_op jit(solution)/shard_map/ppermute | solution.py:282
  40.6 1.9 %collective-permute-start.5 = (bf16[2,512,384]{2,1,0:T(8,128)(2,1)S(1)}, bf16[2,512,384]{2,1,0:T(8,128)(2,1)S(1)}, u32[]{:S(2)}, u32[]{:S(2)}) collective-permute-start(bf16[2,512,384]{2,1,0:T(8,128)(2,1)S(1)} %get-tuple-element.36), channel_id=1, source_target_pairs={{0,8},{8,16},{16,24},{1,9},{9,17},{17,25},{2,10},{10,18},{18,26},{... | collective-permute-start | bytes 2359304 | tf_op jit(solution)/shard_map/ppermute | solution.py:282
  42.5 3.8 %collective-permute-start.4 = (bf16[1,384,384]{2,1,0:T(8,128)(2,1)S(1)}, bf16[1,384,384]{2,1,0:T(8,128)(2,1)S(1)}, u32[]{:S(2)}, u32[]{:S(2)}) collective-permute-start(bf16[1,384,384]{2,1,0:T(8,128)(2,1)S(1)} %shard_map.72.refs_4_), channel_id=1, source_target_pairs={{0,5},{1,4},{2,7},{3,6},{4,1},{5,0},{6,3},{7,2},{8,13},{9,12},{10,... | collective-permute-start | bytes 884744 | tf_op jit(solution)/shard_map/ppermute | solution.py:290
  46.3 0.0 collective-permute-start.3
  46.3 20.0 %collective-permute-done.5.low_ref = bf16[2,512,384]{2,1,0:T(8,128)(2,1)S(1)} collective-permute-done((bf16[2,512,384]{2,1,0:T(8,128)(2,1)S(1)}, bf16[2,512,384]{2,1,0:T(8,128)(2,1)S(1)}, u32[]{:S(2)}, u32[]{:S(2)}) %collective-permute-start.5) | collective-permute-done | bytes 786464 | tf_op jit(solution)/shard_map/ppermute | solution.py:282
  66.3 1.5 %shard_map.74 = (bf16[1,384,384]{2,1,0:T(8,128)(2,1)S(1)}, bf16[1,384,384]{2,1,0:T(8,128)(2,1)S(1)}) custom-call(s32[24]{0:T(128)S(1)} %pad_add_fusion.local.task, s32[1]{0:T(128)} %bitcast.me, bf16[8,512,384]{2,1,0:T(8,128)(2,1)S(1)} %get-tuple-element.34.x_ref, bf16[8,384,512]{2,1,0:T(8,128)(2,1)S(1)} %get-tuple-element.35.y_ref, ...), custom_call_target="tpu_custom_call" | custom-call | flops 603979776 | bytes 2949120 | tf_op jit(solution)/shard_map/pallas_call | solution.py:225
  67.9 0.1 collective-permute-start.6
  67.9 2.7 %collective-permute-start.7 = (bf16[1,384,384]{2,1,0:T(8,128)(2,1)S(1)}, bf16[1,384,384]{2,1,0:T(8,128)(2,1)S(1)}, u32[]{:S(2)}, u32[]{:S(2)}) collective-permute-start(bf16[1,384,384]{2,1,0:T(8,128)(2,1)S(1)} %get-tuple-element.38), channel_id=1, source_target_pairs={{0,7},{1,6},{2,5},{3,4},{4,3},{5,2},{6,1},{7,0},{8,15},{9,14},{10,... | collective-permute-start | bytes 884744 | tf_op jit(solution)/shard_map/ppermute | solution.py:290
  70.6 0.0 collective-permute-done.8.low_ref
  70.6 2.4 %shard_map.75 = (bf16[1,384,384]{2,1,0:T(8,128)(2,1)S(1)}, bf16[1,384,384]{2,1,0:T(8,128)(2,1)S(1)}, bf16[1,384,384]{2,1,0:T(8,128)(2,1)S(1)}, bf16[1,384,384]{2,1,0:T(8,128)(2,1)S(1)}) custom-call(s32[24]{0:T(128)S(1)} %pad_add_fusion.local.task, s32[1]{0:T(128)} %bitcast.me, bf16[8,512,384]{2,1,0:T(8,128)(2,1)S(1)} %get-tuple-element.34.x_ref, ...), custom_call_target="tpu_custom_call" | custom-call | flops 1207959552 | bytes 5898240 | tf_op jit(solution)/shard_map/pallas_call | solution.py:225
  73.0 3.4 %collective-permute-start.10 = (bf16[1,384,384]{2,1,0:T(8,128)(2,1)S(1)}, bf16[1,384,384]{2,1,0:T(8,128)(2,1)S(1)}, u32[]{:S(2)}, u32[]{:S(2)}) collective-permute-start(bf16[1,384,384]{2,1,0:T(8,128)(2,1)S(1)} %get-tuple-element.41), channel_id=1, source_target_pairs={{0,2},{1,3},{2,0},{3,1},{4,6},{5,7},{6,4},{7,5},{8,10},{9,11},{10,... | collective-permute-start | bytes 884744 | tf_op jit(solution)/shard_map/ppermute | solution.py:290
  76.4 0.0 collective-permute-done.4.refs_1_
  76.4 0.8 collective-permute-start.11
  77.1 7.3 %collective-permute-done.3.refs_0_ = bf16[1,384,384]{2,1,0:T(8,128)(2,1)S(1)} collective-permute-done((bf16[1,384,384]{2,1,0:T(8,128)(2,1)S(1)}, bf16[1,384,384]{2,1,0:T(8,128)(2,1)S(1)}, u32[]{:S(2)}, u32[]{:S(2)}) %collective-permute-start.3) | collective-permute-done | bytes 294944 | tf_op jit(solution)/shard_map/ppermute | solution.py:290
  84.5 2.2 %collective-permute-start.9 = (bf16[1,384,384]{2,1,0:T(8,128)(2,1)S(1)}, bf16[1,384,384]{2,1,0:T(8,128)(2,1)S(1)}, u32[]{:S(2)}, u32[]{:S(2)}) collective-permute-start(bf16[1,384,384]{2,1,0:T(8,128)(2,1)S(1)} %get-tuple-element.40), channel_id=1, source_target_pairs={{0,3},{1,2},{2,1},{3,0},{4,7},{5,6},{6,5},{7,4},{8,11},{9,10},{10,... | collective-permute-start | bytes 884744 | tf_op jit(solution)/shard_map/ppermute | solution.py:290
  86.7 4.6 %collective-permute-done.6.refs_2_ = bf16[1,384,384]{2,1,0:T(8,128)(2,1)S(1)} collective-permute-done((bf16[1,384,384]{2,1,0:T(8,128)(2,1)S(1)}, bf16[1,384,384]{2,1,0:T(8,128)(2,1)S(1)}, u32[]{:S(2)}, u32[]{:S(2)}) %collective-permute-start.6) | collective-permute-done | bytes 294944 | tf_op jit(solution)/shard_map/ppermute | solution.py:290
  91.2 9.3 %collective-permute-done.7.refs_3_ = bf16[1,384,384]{2,1,0:T(8,128)(2,1)S(1)} collective-permute-done((bf16[1,384,384]{2,1,0:T(8,128)(2,1)S(1)}, bf16[1,384,384]{2,1,0:T(8,128)(2,1)S(1)}, u32[]{:S(2)}, u32[]{:S(2)}) %collective-permute-start.7) | collective-permute-done | bytes 294944 | tf_op jit(solution)/shard_map/ppermute | solution.py:290
  100.6 0.0 collective-permute-done.10.refs_5_
  100.6 0.0 collective-permute-done.11.refs_6_
  100.6 0.0 collective-permute-done.9.refs_4_
  100.6 1.5 %shard_map.76 = bf16[8,384,384]{2,1,0:T(8,128)(2,1)} custom-call(s32[1]{0:T(128)} %bitcast.me, bf16[1,384,384]{2,1,0:T(8,128)(2,1)S(1)} %collective-permute-done.3.refs_0_, bf16[1,384,384]{2,1,0:T(8,128)(2,1)S(1)} %collective-permute-done.4.refs_1_, bf16[1,384,384]{2,1,0:T(8,128)(2,1)S(1)} %collective-permute-done.6.refs_2_, ...), custom_call_target="tpu_custom_call" | custom-call | bytes 4718592 | tf_op jit(solution)/shard_map/pallas_call | solution.py:254
Async XLA Ops:
  1.4 5.8 %collective-permute-start = (s32[24]{0:T(128)S(1)}, s32[24]{0:T(128)S(1)}, u32[]{:S(2)}, u32[]{:S(2)}) collective-permute-start(s32[24]{0:T(128)S(1)} %pad_add_fusion.local.task), channel_id=1, source_target_pairs={{8,0},{16,8},{24,16},{9,1},{17,9},{25,17},{10,2},{18,10},{26,18},{... | collective-permute-start | bytes 296 | tf_op jit(solution)/shard_map/ppermute | solution.py:277
  16.6 6.8 %collective-permute-start.2 = (bf16[1,512,384]{2,1,0:T(8,128)(2,1)S(1)}, bf16[1,512,384]{2,1,0:T(8,128)(2,1)S(1)}, u32[]{:S(2)}, u32[]{:S(2)}) collective-permute-start(bf16[1,512,384]{2,1,0:T(8,128)(2,1)S(1)} %get-tuple-element.32), channel_id=1, source_target_pairs={{0,8},{8,16},{16,24},{1,9},{9,17},{17,25},{2,10},{10,18},{18,26},{... | collective-permute-start | bytes 1179656 | tf_op jit(solution)/shard_map/ppermute | solution.py:282
  18.7 8.9 %collective-permute-start.1 = (bf16[1,512,384]{2,1,0:T(8,128)(2,1)S(1)}, bf16[1,512,384]{2,1,0:T(8,128)(2,1)S(1)}, u32[]{:S(2)}, u32[]{:S(2)}) collective-permute-start(bf16[1,512,384]{2,1,0:T(8,128)(2,1)S(1)} %get-tuple-element.31), channel_id=1, source_target_pairs={{0,8},{8,16},{16,24},{1,9},{9,17},{17,25},{2,10},{10,18},{18,26},{... | collective-permute-start | bytes 1179656 | tf_op jit(solution)/shard_map/ppermute | solution.py:282
  37.4 33.2 %collective-permute-start.8 = (bf16[4,512,384]{2,1,0:T(8,128)(2,1)S(1)}, bf16[4,512,384]{2,1,0:T(8,128)(2,1)S(1)}, u32[]{:S(2)}, u32[]{:S(2)}) collective-permute-start(bf16[4,512,384]{2,1,0:T(8,128)(2,1)S(1)} %get-tuple-element.39), channel_id=1, source_target_pairs={{0,8},{8,16},{16,24},{1,9},{9,17},{17,25},{2,10},{10,18},{18,26},{... | collective-permute-start | bytes 4718600 | tf_op jit(solution)/shard_map/ppermute | solution.py:282
  40.6 25.8 %collective-permute-start.5 = (bf16[2,512,384]{2,1,0:T(8,128)(2,1)S(1)}, bf16[2,512,384]{2,1,0:T(8,128)(2,1)S(1)}, u32[]{:S(2)}, u32[]{:S(2)}) collective-permute-start(bf16[2,512,384]{2,1,0:T(8,128)(2,1)S(1)} %get-tuple-element.36), channel_id=1, source_target_pairs={{0,8},{8,16},{16,24},{1,9},{9,17},{17,25},{2,10},{10,18},{18,26},{... | collective-permute-start | bytes 2359304 | tf_op jit(solution)/shard_map/ppermute | solution.py:282
  42.5 33.9 %collective-permute-start.4 = (bf16[1,384,384]{2,1,0:T(8,128)(2,1)S(1)}, bf16[1,384,384]{2,1,0:T(8,128)(2,1)S(1)}, u32[]{:S(2)}, u32[]{:S(2)}) collective-permute-start(bf16[1,384,384]{2,1,0:T(8,128)(2,1)S(1)} %shard_map.72.refs_4_), channel_id=1, source_target_pairs={{0,5},{1,4},{2,7},{3,6},{4,1},{5,0},{6,3},{7,2},{8,13},{9,12},{10,... | collective-permute-start | bytes 884744 | tf_op jit(solution)/shard_map/ppermute | solution.py:290
  46.3 38.2 %collective-permute-start.3 = (bf16[1,384,384]{2,1,0:T(8,128)(2,1)S(1)}, bf16[1,384,384]{2,1,0:T(8,128)(2,1)S(1)}, u32[]{:S(2)}, u32[]{:S(2)}) collective-permute-start(bf16[1,384,384]{2,1,0:T(8,128)(2,1)S(1)} %shard_map.71.refs_3_), channel_id=1, source_target_pairs={{0,4},{1,5},{2,6},{3,7},{4,0},{5,1},{6,2},{7,3},{8,12},{9,13},{10,... | collective-permute-start | bytes 884744 | tf_op jit(solution)/shard_map/ppermute | solution.py:290
  67.9 23.4 %collective-permute-start.6 = (bf16[1,384,384]{2,1,0:T(8,128)(2,1)S(1)}, bf16[1,384,384]{2,1,0:T(8,128)(2,1)S(1)}, u32[]{:S(2)}, u32[]{:S(2)}) collective-permute-start(bf16[1,384,384]{2,1,0:T(8,128)(2,1)S(1)} %get-tuple-element.37), channel_id=1, source_target_pairs={{0,6},{1,7},{2,4},{3,5},{4,2},{5,3},{6,0},{7,1},{8,14},{9,15},{10,... | collective-permute-start | bytes 884744 | tf_op jit(solution)/shard_map/ppermute | solution.py:290
  67.9 32.6 %collective-permute-start.7 = (bf16[1,384,384]{2,1,0:T(8,128)(2,1)S(1)}, bf16[1,384,384]{2,1,0:T(8,128)(2,1)S(1)}, u32[]{:S(2)}, u32[]{:S(2)}) collective-permute-start(bf16[1,384,384]{2,1,0:T(8,128)(2,1)S(1)} %get-tuple-element.38), channel_id=1, source_target_pairs={{0,7},{1,6},{2,5},{3,4},{4,3},{5,2},{6,1},{7,0},{8,15},{9,14},{10,... | collective-permute-start | bytes 884744 | tf_op jit(solution)/shard_map/ppermute | solution.py:290
  73.0 27.6 %collective-permute-start.10 = (bf16[1,384,384]{2,1,0:T(8,128)(2,1)S(1)}, bf16[1,384,384]{2,1,0:T(8,128)(2,1)S(1)}, u32[]{:S(2)}, u32[]{:S(2)}) collective-permute-start(bf16[1,384,384]{2,1,0:T(8,128)(2,1)S(1)} %get-tuple-element.41), channel_id=1, source_target_pairs={{0,2},{1,3},{2,0},{3,1},{4,6},{5,7},{6,4},{7,5},{8,10},{9,11},{10,... | collective-permute-start | bytes 884744 | tf_op jit(solution)/shard_map/ppermute | solution.py:290
  76.4 24.2 %collective-permute-start.11 = (bf16[1,384,384]{2,1,0:T(8,128)(2,1)S(1)}, bf16[1,384,384]{2,1,0:T(8,128)(2,1)S(1)}, u32[]{:S(2)}, u32[]{:S(2)}) collective-permute-start(bf16[1,384,384]{2,1,0:T(8,128)(2,1)S(1)} %get-tuple-element.42), channel_id=1, source_target_pairs={{0,1},{1,0},{2,3},{3,2},{4,5},{5,4},{6,7},{7,6},{8,9},{9,8},{10,11... | collective-permute-start | bytes 884744 | tf_op jit(solution)/shard_map/ppermute | solution.py:290
  84.5 16.1 %collective-permute-start.9 = (bf16[1,384,384]{2,1,0:T(8,128)(2,1)S(1)}, bf16[1,384,384]{2,1,0:T(8,128)(2,1)S(1)}, u32[]{:S(2)}, u32[]{:S(2)}) collective-permute-start(bf16[1,384,384]{2,1,0:T(8,128)(2,1)S(1)} %get-tuple-element.40), channel_id=1, source_target_pairs={{0,3},{1,2},{2,1},{3,0},{4,7},{5,6},{6,5},{7,4},{8,11},{9,10},{10,... | collective-permute-start | bytes 884744 | tf_op jit(solution)/shard_map/ppermute | solution.py:290
